TPU v7x, 128 devices: a whole 4x4x4 slice. The times are simulated.
128 devices in a mesh: rep: 2 (over core), tensor: 64 (over x, z, y).
Axes of the slice: x: 4, y: 4, z: 4, core: 2. Of those that a mesh axis runs over, the one named last changes fastest.
Arguments:
- amplitudes: bfloat16 [4, 1600, 3200], P('rep', 'tensor'), may hold values from -6 to 6
- intermediate: bfloat16 [128, 200, 6400], P('tensor', None, 'rep'), may hold values from -0.21875 to 0.21875
- occ_irrep: int32 [200], replicated, may hold values from 0 to 7
- i_window: int32 [16], replicated, may hold values from 0 to 199
- j_window: int32 [128], replicated, may hold values from 0 to 199
- k_window: int32 [4], replicated, may hold values from 0 to 199
- occ_energy: float32 [200], replicated, may hold values from -1 to -0.3
- virt_energy: float32 [1600], replicated, may hold values from 0.2 to 3
Outputs:
- update: bfloat16 [16, 1600, 25600], P('rep', 'tensor')
Inputs may be any that keep to these rules, and one draw needn't show every extreme that they name: `i_window`: occupied orbital numbers, repeats possible. `j_window`: occupied orbital numbers, repeats possible. `k_window`: occupied orbital numbers, repeats possible.
All inputs are finite; a program needn't handle non-finite values.
Results may differ from a plain program's by a relative error of at most 0.0058.
Values may be sent and summed in bfloat16 or wider, within the bound.
A program may use at most 320 MiB of HBM per device.

v0:
```python
import jax
import jax.numpy as jnp
from jax import lax
from jax.sharding import PartitionSpec as P

IRREPS = 8


def arrange_blocks(w_local, sym_cols, irreps, width):
    n_cols = w_local.shape[0] * w_local.shape[1]
    count = w_local.shape[2] // (irreps * width)
    shaped = w_local.reshape(n_cols, count, irreps, width)
    block_index = jnp.bitwise_xor(jnp.arange(irreps, dtype=jnp.int32)[:, None], sym_cols[None, :])
    k_index = jnp.arange(count, dtype=jnp.int32)[None, :]
    picked = shaped[:, k_index, block_index]
    picked = picked.transpose(1, 2, 3, 0)
    return picked.reshape(irreps, count * width, n_cols)


def block_product(left_rows, right_blocks, first_row, sym_value, width, irreps):
    length = left_rows.shape[0]
    depth = left_rows.shape[1]
    n_cols = right_blocks.shape[2]
    offset = first_row % width
    blocks = (length + 2 * width - 2) // width
    padded = jnp.zeros((blocks * width, depth), left_rows.dtype)
    padded = lax.dynamic_update_slice(padded, left_rows, (offset, jnp.zeros((), offset.dtype)))
    labels = jnp.arange(blocks, dtype=jnp.int32)
    targets = jnp.bitwise_xor(jnp.minimum(labels, irreps - 1), sym_value)
    rights = right_blocks[targets]
    product = jnp.einsum(
        "bwk,bkn->bwn",
        padded.reshape(blocks, width, depth),
        rights,
        preferred_element_type=jnp.float32,
    )
    return lax.dynamic_slice_in_dim(product.reshape(blocks * width, n_cols), offset, length, 0)


def make_worker(arranged, sym_rows, groups, width, irreps):

    def worker(block_rows, first_row):
        k_count = block_rows.shape[0]
        length = block_rows.shape[1]
        members = block_rows.shape[2] // width
        k_step = k_count // groups
        results = []
        for member in range(members):
            member_rows = block_rows[:, :, member * width : (member + 1) * width]
            left_rows = member_rows
            left_rows = left_rows.transpose(1, 0, 2).reshape(length, k_step * width)
            product = block_product(left_rows, arranged, first_row, sym_rows[member], width, irreps)
            summed = lax.optimization_barrier(product.astype(jnp.bfloat16)).astype(jnp.float32)
            results.append(summed.astype(jnp.bfloat16))
        return jnp.stack(results)

    return worker


def per_device(
    amplitudes, intermediate, occ_irrep, i_window, j_window, k_window, occ_energy, virt_energy
):
    irreps = IRREPS
    width = virt_energy.shape[0] // irreps
    batch_i = i_window.shape[0]
    k_local = amplitudes.shape[0]
    replica = lax.axis_index("rep")
    column = lax.axis_index("tensor")
    half_i = batch_i // lax.axis_size("rep")
    own_i = lax.dynamic_slice_in_dim(i_window, replica * half_i, half_i)
    rows_sym = occ_irrep[i_window]
    cols_sym = occ_irrep[lax.dynamic_slice_in_dim(k_window, replica * k_local, k_local)]
    groups = 1
    arranged = arrange_blocks(intermediate, cols_sym, irreps, width)
    worker = make_worker(arranged, rows_sym, groups, width, irreps)
    gathered = worker(lax.all_gather(amplitudes, "tensor", axis=1, tiled=True), jnp.int32(0))
    term = lax.optimization_barrier(gathered).astype(jnp.float32)
    summed = lax.psum_scatter(term.astype(jnp.bfloat16), "rep", scatter_dimension=0, tiled=True)
    returned = lax.all_to_all(summed, "tensor", split_axis=1, concat_axis=2, tiled=True)
    rows_local = returned.shape[1]
    j_total = j_window.shape[0]
    shaped = returned.reshape(half_i, rows_local, j_total, width)
    sym_i = occ_irrep[own_i]
    energy_i = occ_energy[own_i]
    sym_j = occ_irrep[j_window]
    energy_j = occ_energy[j_window]
    energy_a = lax.dynamic_slice_in_dim(virt_energy, column * rows_local, rows_local)
    irrep_a = (column * rows_local + jnp.arange(rows_local, dtype=jnp.int32)) // width
    irrep_b = jnp.bitwise_xor(
        jnp.bitwise_xor(irrep_a[None, :, None], sym_i[:, None, None]), sym_j[None, None, :]
    )
    energy_table = virt_energy.reshape(irreps, width)
    energy_b = jnp.zeros(irrep_b.shape + (width,), jnp.float32)
    for label in range(irreps):
        energy_b = jnp.where(
            irrep_b[..., None] == label, energy_table[label][None, None, None, :], energy_b
        )
    denominator = (
        energy_i[:, None, None, None]
        + energy_j[None, None, :, None]
        - energy_a[None, :, None, None]
        - energy_b
    )
    result = (shaped.astype(jnp.float32) / denominator).astype(jnp.bfloat16)
    return result.reshape(half_i, rows_local, j_total * width)


def solution(mesh):
    return jax.shard_map(
        per_device,
        mesh=mesh,
        in_specs=(P("rep", "tensor", None), P("tensor", None, "rep"), P(), P(), P(), P(), P(), P()),
        out_specs=P("rep", "tensor", None),
        check_vma=False,
    )
```

profile of v0, /device:TPU:1, one launch (start us, length us, event | category | flops | bytes accessed | tf_op | source)
XLA Modules:
  0.0 842.5 jit_solution(1066107681700497681)
XLA Ops:
  10.1 11.8 %reshape.557 = bf16[400,2,8,200]{3,2,1,0:T(8,128)(2,1)} reshape(bf16[2,200,3200]{2,1,0:T(8,128)(2,1)} %param.9) | data formatting | bytes 5120000 | tf_op jit(solution)/shard_map/reshape | solution.py:12
  90.0 39.4 %all-gather.2.cloned.1.call-done = bf16[2,1600,3200]{2,0,1:T(2,128)(2,1)} async-done(((bf16[2,25,3200]{2,0,1:T(2,128)(2,1)}), bf16[2,1600,3200]{2,0,1:T(2,128)(2,1)}) %all-gather.2.cloned.1.call-update) | async-done | bytes 20480016 | tf_op jit(solution)/shard_map/all_gather | solution.py:76
  129.4 47.1 %fusion.19 = (bf16[2,1600,200]{2,0,1:T(2,128)(2,1)S(1)}, bf16[2,1600,200]{2,0,1:T(2,128)(2,1)}, bf16[2,1600,200]{2,0,1:T(2,128)(2,1)}, bf16[2,1600,200]{2,0,1:T(...) fusion(bf16[2,1600,3200]{2,0,1:T(2,128)(2,1)} %all-gather.2.clo, ...), kind=kLoop, calls=%fused_computation.130 | loop fusion | bytes 40960000 | tf_op jit(solution)/shard_map/slice | solution.py:49
  231.5 5.4 copy.121
  273.5 5.3 copy.124
  329.3 5.4 copy.128
  371.3 5.3 copy.131
  416.6 33.4 %reduce-scatter.5.cloned.1.call-done = bf16[8,1600,400]{1,2,0:T(8,128)(2,1)} async-done(((bf16[16,1600,400]{1,2,0:T(8,128)(2,1)}), bf16[8,1600,400]{1,2,0:T(8,128)(2,1)}) %reduce-scatter.5.cloned.1.call-update) | async-done | bytes 10240016
  450.0 20.0 %copy.115 = bf16[8,1600,400]{2,0,1:T(8,128)(2,1)} copy(bf16[8,1600,400]{1,2,0:T(8,128)(2,1)} %reduce-scatter.5.cloned.1.call-done) | data formatting | bytes 20480000 | tf_op jit(solution)/shard_map/reduce_scatter | solution.py:78
  470.0 10.5 %all-to-all-start = ((bf16[8,1600,400]{2,0,1:T(8,128)(2,1)}), bf16[8,1600,400]{2,0,1:T(8,128)(2,1)}, u32[]{:S(2)}, u32[]{:S(2)}) async-start(bf16[8,1600,400]{2,0,1:T(8,128)(2,1)} %copy.115), calls=%async_computation | async-start | bytes 26214400 | tf_op jit(solution)/shard_map/all_to_all | solution.py:79
  484.8 9.1 %sub.36 = f32[8,25,128,200]{3,2,0,1:T(8,128)} broadcast(f32[8,25,128]{2,0,1:T(8,128)S(1)} %broadcast_subtract_fusion), dimensions={0,1,2} | broadcast | bytes 20582400 | tf_op jit(solution)/shard_map/sub | solution.py:99
  493.8 25.1 %sub.37 = f32[8,25,25600]{2,0,1:T(8,128)} reshape(f32[8,25,128,200]{3,2,0,1:T(8,128)} %sub.36) | data formatting | bytes 40960000 | tf_op jit(solution)/shard_map/sub | solution.py:99
  519.2 5.6 broadcast_in_dim.195
  524.8 23.6 %broadcast_in_dim.196 = pred[8,25,25600]{2,0,1:T(8,128)(4,1)} reshape(pred[8,25,128,200]{3,2,0,1:T(8,128)(4,1)} %broadcast_in_dim.195) | data formatting | bytes 10240000 | tf_op jit(solution)/shard_map/jit(_where)/broadcast_in_dim | solution.py:95
  548.4 5.5 broadcast_in_dim.200
  553.9 23.6 %broadcast_in_dim.201 = pred[8,25,25600]{2,0,1:T(8,128)(4,1)} reshape(pred[8,25,128,200]{3,2,0,1:T(8,128)(4,1)} %broadcast_in_dim.200) | data formatting | bytes 10240000 | tf_op jit(solution)/shard_map/jit(_where)/broadcast_in_dim | solution.py:95
  577.5 5.5 broadcast_in_dim.205
  583.0 23.7 %broadcast_in_dim.206 = pred[8,25,25600]{2,0,1:T(8,128)(4,1)} reshape(pred[8,25,128,200]{3,2,0,1:T(8,128)(4,1)} %broadcast_in_dim.205) | data formatting | bytes 10240000 | tf_op jit(solution)/shard_map/jit(_where)/broadcast_in_dim | solution.py:95
  606.7 5.5 broadcast_in_dim.210
  612.2 23.6 %broadcast_in_dim.211 = pred[8,25,25600]{2,0,1:T(8,128)(4,1)} reshape(pred[8,25,128,200]{3,2,0,1:T(8,128)(4,1)} %broadcast_in_dim.210) | data formatting | bytes 10240000 | tf_op jit(solution)/shard_map/jit(_where)/broadcast_in_dim | solution.py:95
  635.8 5.5 broadcast_in_dim.215
  641.3 23.6 %broadcast_in_dim.216 = pred[8,25,25600]{2,0,1:T(8,128)(4,1)} reshape(pred[8,25,128,200]{3,2,0,1:T(8,128)(4,1)} %broadcast_in_dim.215) | data formatting | bytes 10240000 | tf_op jit(solution)/shard_map/jit(_where)/broadcast_in_dim | solution.py:95
  664.9 5.5 broadcast_in_dim.220
  670.4 23.6 %broadcast_in_dim.221 = pred[8,25,25600]{2,0,1:T(8,128)(4,1)} reshape(pred[8,25,128,200]{3,2,0,1:T(8,128)(4,1)} %broadcast_in_dim.220) | data formatting | bytes 10240000 | tf_op jit(solution)/shard_map/jit(_where)/broadcast_in_dim | solution.py:95
  694.0 5.5 broadcast_in_dim.225
  699.5 23.8 %broadcast_in_dim.226 = pred[8,25,25600]{2,0,1:T(8,128)(4,1)} reshape(pred[8,25,128,200]{3,2,0,1:T(8,128)(4,1)} %broadcast_in_dim.225) | data formatting | bytes 10240000 | tf_op jit(solution)/shard_map/jit(_where)/broadcast_in_dim | solution.py:95
  723.3 5.5 broadcast_in_dim.230
  728.8 23.6 %broadcast_in_dim.231 = pred[8,25,25600]{2,0,1:T(8,128)(4,1)} reshape(pred[8,25,128,200]{3,2,0,1:T(8,128)(4,1)} %broadcast_in_dim.230) | data formatting | bytes 10240000 | tf_op jit(solution)/shard_map/jit(_where)/broadcast_in_dim | solution.py:95
  753.7 7.6 convert_bitcast_fusion
  761.3 17.6 %copy.116 = f32[8,25,64,400]{3,2,0,1:T(8,128)} copy(f32[8,25,64,400]{3,0,1,2:T(8,128)S(1)} %convert_bitcast_fusion) | data formatting | bytes 40960000 | tf_op jit(solution)/shard_map/convert_element_type | solution.py:104
  779.0 23.8 %reshape.589 = f32[8,25,25600]{2,0,1:T(8,128)} reshape(f32[8,25,64,400]{3,2,0,1:T(8,128)} %copy.116) | data formatting | bytes 40960000 | tf_op jit(solution)/shard_map/convert_element_type | solution.py:104
  802.7 32.6 %divide_convert_fusion = bf16[8,25,25600]{2,0,1:T(8,128)(2,1)} fusion(f32[8,25,25600]{2,0,1:T(8,128)} %reshape.589, f32[8,25,25600]{2,0,1:T(8,128)} %sub.37, pred[8,25,25600]{2,0,1:T(8,128)(4,1)} %broadcast_in_dim.196, pred[8,25,25600]{2,0,1:T(8,128)(4,1)} %broadcast_in_dim.201, pred[8,25,25600]{2,0,1:T(8,128)(4,1)} %broadcast_in_dim.206, ...), kind=kLoop, calls=%fused_computation.24 | loop fusion | flops 56320000 | bytes 92979200 | tf_op jit(solution)/shard_map/convert_element_type | solution.py:104
  (237 shorter events, 295.4 us)
Async XLA Ops:
  6.5 1.4 copy-start
  6.5 122.9 %all-gather.2.cloned.1.call-start = ((), (), s32[]{:S(2)}) async-start(), calls=%async_computation.2 | async-start | bytes 20800000 | tf_op jit(solution)/shard_map/all_gather | solution.py:76
  7.3 442.8 %reduce-scatter.5.cloned.1.call-start = ((), (), s32[]{:S(2)}) async-start(), calls=%async_computation.3 | async-start | bytes 31948800
  188.9 2.6 copy-start.2
  395.2 2.9 copy-start.3
  398.1 1.8 copy-start.4
  398.1 3.0 copy-start.5
  399.9 2.4 copy-start.6
  401.1 2.4 copy-start.7
  402.3 2.4 copy-start.8
  403.5 2.5 copy-start.9
  404.7 2.4 copy-start.10
  405.9 2.3 copy-start.11
  407.1 2.4 copy-start.12
  408.3 2.4 copy-start.13
  409.5 2.4 copy-start.14
  410.7 2.3 copy-start.15
  411.9 2.4 copy-start.16
  413.0 2.4 copy-start.17
  470.0 10.5 %copy-start.19 = (s32[16]{0:T(128)S(1)}, s32[16]{0:T(128)}, u32[]{:S(2)}) copy-start(s32[16]{0:T(128)} %param.11) | copy-start | bytes 196
  470.0 10.6 %copy-start.20 = (s32[128]{0:T(128)S(1)}, s32[128]{0:T(128)}, u32[]{:S(2)}) copy-start(s32[128]{0:T(128)} %param.12) | copy-start | bytes 1540
  470.0 11.3 %copy-start.1 = (f32[200]{0:T(256)S(1)}, f32[200]{0:T(256)}, u32[]{:S(2)}) copy-start(f32[200]{0:T(256)} %param.14) | copy-start | bytes 2404
  470.0 14.5 %copy-start.18 = (f32[1600]{0:T(1024)S(1)}, f32[1600]{0:T(1024)}, u32[]{:S(2)}) copy-start(f32[1600]{0:T(1024)} %param.15) | copy-start | bytes 19204
  470.0 283.7 %all-to-all-start = ((bf16[8,1600,400]{2,0,1:T(8,128)(2,1)}), bf16[8,1600,400]{2,0,1:T(8,128)(2,1)}, u32[]{:S(2)}, u32[]{:S(2)}) async-start(bf16[8,1600,400]{2,0,1:T(8,128)(2,1)} %copy.115), calls=%async_computation | async-start | bytes 26214400 | tf_op jit(solution)/shard_map/all_to_all | solution.py:79
Sparse Core Ops, SparseCore 0:
  10.2 119.1 all-gather.1
  416.7 33.2 reduce-scatter.4
where the time goes:
time: 851 us; the launch traced here: 842 us
  local copies, waits for them, and re-layouts  641 us (75%)
  waiting for transfers between devices  73.5 us (9%)
  other arithmetic  52.4 us (6%)
  matrix products  50.6 us (6%)
  between operations  14.6 us (2%)
  starting transfers between devices  10.5 us (1%)
    broadcast_in_dim x32, local copies, waits for them, and re-layouts, per_device(): jnp.where(irrep_b[..., None] == label, energy_table[label][None, None, No...  234 us
    unnamed x89, local copies, waits for them, and re-layouts  144 us
    dot_general x16, matrix products, block_product(): jnp.einsum('bwk,bkn->bwn', padded.reshape(blocks, width, depth), rights,...  50.6 us
    slice x1, local copies, waits for them, and re-layouts, worker(): member_rows = block_rows[:, :, member * width:(member + 1) * width]  47.1 us
    gather x16, local copies, waits for them, and re-layouts, block_product(): rights = right_blocks[targets]  46.5 us
    convert_element_type x2, local copies, waits for them, and re-layouts, per_device(): result = (shaped.astype(jnp.float32) / denominator).astype(jnp.bfloat16)  41.4 us
    convert_element_type x2, other arithmetic, per_device(): result = (shaped.astype(jnp.float32) / denominator).astype(jnp.bfloat16)  40.2 us
    all_gather x1, waiting for transfers between devices, per_device(): lax.all_gather(amplitudes, 'tensor', axis=1, tiled=True)  39.4 us
  transfers between devices with their start and end apart: 3, of which 2 were waited for; matrix products, arithmetic and copies ran while one was open for 42% of the time, Pallas kernels for 0%

commit v1 on v0

v1 whole, which is shorter than its diff:
```python
import functools
import jax
import jax.numpy as jnp
from jax import lax
from jax.experimental import pallas as pl
from jax.experimental.pallas import tpu as pltpu
from jax.sharding import PartitionSpec as P

IRREPS = 8
VH = 200
ROWS = 25
HALF = 8
PLANE = 16
RING = 4
COLS = 400
LANES = 128
MAIN = 384
TILES = 13
WIN = TILES * LANES
PIECES = 79
PAD = 64
BLOCK = 64
MESH = pl.DeviceIdType.MESH
F32 = jnp.float32
BF16 = jnp.bfloat16
ORDER = (
    (0, 1, 2, 3, 4, 5, 10, 11, 12, 6, 7, 8, 9),
    (4, 5, 0, 1, 2, 3, 6, 7, 8, 9, 10, 11, 12),
    (7, 8, 4, 5, 6, 9, 10, 11, 12, 0, 1, 2, 3),
    (10, 11, 12, 7, 8, 9, 0, 1, 2, 3, 4, 5, 6),
)


def pack_kernel(sk_ref, w_ref, a_ref, wm_ref, wr_ref, am_ref, rows, last, rest):
    for k in range(2):
        for h in range(IRREPS):
            first = (k * IRREPS + h) * VH
            g = jnp.bitwise_xor(sk_ref[k], h)
            if k == 0:
                wm_ref[g, :, 0:VH] = w_ref[:, first : first + VH]
            else:
                wm_ref[g, :, VH:MAIN] = w_ref[:, first : first + MAIN - VH]
                wr_ref[:, h * 16 : (h + 1) * 16] = w_ref[:, first + MAIN - VH : first + VH]
    for half in range(2):
        rest[...] = jnp.zeros_like(rest)
        for i in range(HALF):
            first = (half * HALF + i) * VH
            rows[0:ROWS, 0:VH] = a_ref[0, :, first : first + VH].astype(F32)
            rows[0:ROWS, VH:COLS] = a_ref[1, :, first : first + VH].astype(F32)
            for lt in range(3):
                lanes = slice(lt * LANES, (lt + 1) * LANES)
                am_ref[half, lt * 25 + 3 * i : lt * 25 + 3 * i + 3] = (
                    rows[0:24, lanes].reshape(3, 8, LANES).astype(BF16)
                )
                last[lt, i : i + 1, :] = rows[24:25, lanes]
            rest[0:ROWS, i * 16 : (i + 1) * 16] = rows[0:ROWS, MAIN:COLS]
        for lt in range(3):
            am_ref[half, lt * 25 + 24] = last[lt].astype(BF16)
        am_ref[half, 75:79] = rest[...].reshape(4, 8, LANES).astype(BF16)


def pack(sk, w, a):
    vm = pl.BlockSpec(memory_space=pltpu.VMEM)
    return pl.pallas_call(
        pack_kernel,
        out_shape=(
            jax.ShapeDtypeStruct((IRREPS, COLS, MAIN), BF16),
            jax.ShapeDtypeStruct((COLS, LANES), BF16),
            jax.ShapeDtypeStruct((2, PIECES, 8, LANES), BF16),
        ),
        in_specs=[pl.BlockSpec(memory_space=pltpu.SMEM), vm, vm],
        out_specs=(vm, vm, vm),
        scratch_shapes=[
            pltpu.VMEM((32, 512), F32),
            pltpu.VMEM((3, 8, LANES), F32),
            pltpu.VMEM((32, LANES), F32),
        ],
        compiler_params=pltpu.CompilerParams(vmem_limit_bytes=40 << 20),
        name="pack",
    )(sk, w, a)


def is_value(y, value):
    return 1 - lax.div(lax.rem(y - value + RING, RING) + RING - 1, RING)


def main_kernel(
    s_ref, wm_ref, wr_ref, am_ref, d_ref, e_ref, o_ref,
    wb, wrb, ab, left, acc, snd,
    sib_send, sib_recv, own_sem, a_send, a_recv,
    w_send, w_recv, f_send, f_recv, o_send, o_recv,
):
    r = lax.axis_index("rep")
    col = lax.axis_index("tensor")
    q = lax.div(col, RING)
    y = lax.rem(col, RING)
    x, z = lax.div(q, 4), lax.rem(q, 4)
    phase = PAD * lax.rem(q, 2)
    sib = (1 - r, col)

    def plane_peer(o):
        px, pz = lax.rem(x + lax.div(o, 4), 4), lax.rem(z + lax.rem(o, 4), 4)
        return px * 4 + pz

    def ring_peer(d):
        return (r, q * RING + lax.rem(y + d, RING))

    barrier = pltpu.get_barrier_semaphore()

    def greet(o, c):
        pl.semaphore_signal(barrier, inc=1, device_id=(r, plane_peer(o) * RING + y), device_id_type=MESH)
        return c

    lax.fori_loop(1, PLANE, greet, 0)
    for d in (1, 2, 3):
        pl.semaphore_signal(barrier, inc=1, device_id=ring_peer(d), device_id_type=MESH)
    pl.semaphore_signal(barrier, inc=1, device_id=sib, device_id_type=MESH)
    pl.semaphore_wait(barrier, PLANE - 1 + 3 + 1)

    def remote(src, dst, ss, rs, dev):
        return pltpu.make_async_remote_copy(
            src_ref=src, dst_ref=dst, send_sem=ss, recv_sem=rs, device_id=dev, device_id_type=MESH
        )

    def w_rows(d):
        first = PAD + COLS * lax.rem(y + RING - d, RING)
        return pl.ds(pl.multiple_of(first, 16), COLS)

    def spot(d, half):
        lanes = pl.ds(pl.multiple_of(MAIN * half, LANES), MAIN)
        rest = pl.ds(pl.multiple_of(LANES * half, LANES), LANES)
        return wb.at[:, w_rows(d), lanes], wrb.at[w_rows(d), rest]

    def w_copies(d):
        dst, dst_r = spot(0, r)
        return (
            remote(wm_ref, dst, w_send.at[d, 0], w_recv.at[d, 0], ring_peer(d)),
            remote(wr_ref, dst_r, w_send.at[d, 1], w_recv.at[d, 1], ring_peer(d)),
        )

    def w_arrivals(d):
        dst, dst_r = spot(d, r)
        return (
            remote(wm_ref, dst, w_send.at[d, 0], w_recv.at[d, 0], ring_peer(d)),
            remote(wr_ref, dst_r, w_send.at[d, 1], w_recv.at[d, 1], ring_peer(d)),
        )

    def forwards(d, half):
        dst, dst_r = spot(d, half)
        src, src_r = (wm_ref, wr_ref) if d == 0 else (dst, dst_r)
        return (
            remote(src, dst, f_send.at[d, 0], f_recv.at[d, 0], sib),
            remote(src_r, dst_r, f_send.at[d, 1], f_recv.at[d, 1], sib),
        )

    a_sib = remote(am_ref.at[1 - r], ab.at[q, r], sib_send, sib_recv, sib)
    a_sib.start()
    a_own = pltpu.make_async_copy(am_ref.at[r], ab.at[q, r], own_sem.at[0])
    a_own.start()
    for d in (1, 3):
        for c in w_copies(d):
            c.start()
    for c in forwards(0, r):
        c.start()
    own_w, own_wr = spot(0, r)
    w_own = pltpu.make_async_copy(wm_ref, own_w, own_sem.at[1])
    w_own.start()
    wr_own = pltpu.make_async_copy(wr_ref, own_wr, own_sem.at[2])
    wr_own.start()
    a_own.wait()
    remote(am_ref.at[r], ab.at[q, 1 - r], sib_send, sib_recv, sib).wait_recv()

    def a_copy(o):
        return remote(ab.at[q], ab.at[q], a_send.at[o], a_recv.at[o], (r, plane_peer(o) * RING + y))

    def a_start(o, c):
        a_copy(o).start()
        return c

    lax.fori_loop(1, PLANE, a_start, 0)

    def a_wait(o, c):
        source = lax.rem(x + 4 - lax.div(o, 4), 4) * 4 + lax.rem(z + 4 - lax.rem(o, 4), 4)
        remote(ab.at[source], ab.at[source], a_send.at[o], a_recv.at[o], sib).wait_recv()
        return c

    lax.fori_loop(1, PLANE, a_wait, 0)

    lane_group = lax.div(lax.broadcasted_iota(jnp.int32, (BLOCK, LANES), 1), 16)

    def build(g, c):
        for i in range(HALF):
            h = jnp.bitwise_xor(g, s_ref[i])
            base = i * BLOCK
            for half in range(2):
                for lt in range(3):
                    lanes = slice(half * MAIN + lt * LANES, half * MAIN + (lt + 1) * LANES)
                    parts = [
                        ab[2 * h + zp, half, lt * 25 + 3 * i : lt * 25 + 3 * i + 3].astype(F32).reshape(24, LANES)
                        for zp in range(2)
                    ] + [ab[2 * h + zp, half, lt * 25 + 24].astype(F32) for zp in range(2)]
                    left[g, base : base + BLOCK, lanes] = jnp.concatenate(parts, axis=0).astype(BF16)
                tails = [ab[2 * h + zp, half, 75:79].astype(F32).reshape(32, LANES) for zp in range(2)]
                parts = [t[0:24] for t in tails] + [jnp.broadcast_to(t[24:25], (8, LANES)) for t in tails]
                tail = jnp.concatenate(parts, axis=0)
                place = jnp.bitwise_xor(g, s_ref[HALF + 2 * half + 1])
                tail = pltpu.roll(tail, lax.rem(16 * (place - i) + LANES, LANES), 1)
                tail = jnp.where(lane_group == place, tail, 0.0)
                lanes = slice(2 * MAIN + half * LANES, 2 * MAIN + (half + 1) * LANES)
                left[g, base : base + BLOCK, lanes] = tail.astype(BF16)
        return c

    lax.fori_loop(0, IRREPS, build, 0)
    w_own.wait()
    wr_own.wait()
    for c in forwards(0, 1 - r):
        c.wait_recv()

    lo, hi = 0, 0
    for value in range(RING):
        picked = is_value(y, value)
        lo = lo + picked * sum(ORDER[value][p] * 16**p for p in range(7))
        hi = hi + picked * sum(ORDER[value][p + 7] * 16**p for p in range(6))
    row_index = lax.broadcasted_iota(jnp.int32, (8, LANES), 0)
    NT = (((1,), (1,)), ((), ()))

    def out_copy(p, t, peer):
        lanes = pl.ds(pl.multiple_of(q * WIN + t * LANES, LANES), LANES)
        return snd.at[p, peer], o_ref.at[:, :, lanes]

    def step(p, carry):
        lo, hi = carry
        t = lax.rem(lo, 16)

        @pl.when(p == 2)
        def _():
            for d in (1, 3):
                for c in w_arrivals(d):
                    c.wait_recv()
                for c in forwards(d, r):
                    c.start()
            for d in (1, 3):
                for c in w_copies(d):
                    c.wait_send()
            for c in w_copies(2):
                c.start()
            for d in (1, 3):
                for c in forwards(d, 1 - r):
                    c.wait_recv()

        @pl.when(p == 9)
        def _():
            for c in w_arrivals(2):
                c.wait_recv()
            for c in forwards(2, r):
                c.start()
            for c in forwards(2, 1 - r):
                c.wait_recv()

        window = pl.ds(pl.multiple_of(t * LANES + PAD - phase, 16), LANES)

        def multiply(g, c):
            total = lax.dot_general(
                left[g, :, 0 : 2 * MAIN], wb[g, window, :], NT, preferred_element_type=F32
            )
            total = total + lax.dot_general(
                left[g, :, 2 * MAIN :], wrb[window, :], NT, preferred_element_type=F32
            )
            acc[g] = total.reshape(HALF, BLOCK, LANES)
            return c

        lax.fori_loop(0, IRREPS, multiply, 0)
        lanes = pl.ds(pl.multiple_of(t * LANES, LANES), LANES)

        def finish(s, c):
            h = 2 * lax.rem(x + lax.div(s, 2), 4) + lax.rem(lax.div(z, 2) + s, 2)
            energy_a = e_ref[h]
            tail = [jnp.zeros((8, LANES), F32), jnp.zeros((8, LANES), F32)]
            for i in range(HALF):
                g = jnp.bitwise_xor(h, s_ref[i])
                den = d_ref[h, i : i + 1, lanes] - energy_a
                value = acc[g, i] / den
                for zp in range(2):
                    snd[p, 2 * h + zp, 3 * i : 3 * i + 3] = (
                        value[24 * zp : 24 * zp + 24].reshape(3, 8, LANES).astype(BF16)
                    )
                    tail[zp] = jnp.where(row_index == i, value[48 + 8 * zp : 56 + 8 * zp], tail[zp])
            for zp in range(2):
                peer = 2 * h + zp
                snd[p, peer, 24] = tail[zp].astype(BF16)
                src, dst = out_copy(p, t, peer)

                @pl.when(peer != q)
                def _():
                    remote(src, dst, o_send.at[peer], o_recv.at[q], (r, peer * RING + y)).start()

                @pl.when(peer == q)
                def _():
                    pltpu.make_async_copy(src, dst, o_send.at[peer]).start()

            return c

        lax.fori_loop(0, IRREPS, finish, 0)
        return lax.div(lo, 16) + lax.rem(hi, 16) * 16**6, lax.div(hi, 16)

    lax.fori_loop(0, TILES, step, (lo, hi))

    a_sib.wait_send()
    for d in range(RING):
        for c in forwards(d, r):
            c.wait_send()
    for c in w_copies(2):
        c.wait_send()

    def drain(o, c):
        a_copy(o).wait_send()
        return c

    lax.fori_loop(1, PLANE, drain, 0)

    def all_tiles(peer):
        lanes = pl.ds(pl.multiple_of(peer * WIN, LANES), WIN)
        return o_ref.at[:, :, lanes]

    def drain_out(o, c):
        peer = plane_peer(o)
        whole = all_tiles(peer)
        remote(whole, whole, o_send.at[peer], o_recv.at[peer], sib).wait_send()
        remote(whole, whole, o_send.at[peer], o_recv.at[peer], sib).wait_recv()
        return c

    lax.fori_loop(1, PLANE, drain_out, 0)
    own = all_tiles(q)
    pltpu.make_async_copy(own, own, o_send.at[q]).wait()


def exchange(symmetry, wm, wr, am, d_table, e_table):
    vm = pl.BlockSpec(memory_space=pltpu.VMEM)
    hbm = pl.BlockSpec(memory_space=pl.ANY)
    dma = pltpu.SemaphoreType.DMA
    return pl.pallas_call(
        main_kernel,
        out_shape=jax.ShapeDtypeStruct((25, 8, PLANE * WIN), BF16),
        in_specs=[pl.BlockSpec(memory_space=pltpu.SMEM), hbm, hbm, hbm, vm, vm],
        out_specs=hbm,
        scratch_shapes=[
            pltpu.VMEM((IRREPS, RING * COLS + 2 * PAD, 2 * MAIN), BF16),
            pltpu.VMEM((RING * COLS + 2 * PAD, 2 * LANES), BF16),
            pltpu.VMEM((PLANE, 2, PIECES, 8, LANES), BF16),
            pltpu.VMEM((IRREPS, HALF * BLOCK, 2 * MAIN + 2 * LANES), BF16),
            pltpu.VMEM((IRREPS, HALF, BLOCK, LANES), F32),
            pltpu.VMEM((TILES, PLANE, 25, 8, LANES), BF16),
            dma, dma, dma((3,)), dma((PLANE,)), dma((PLANE,)),
            dma((RING, 2)), dma((RING, 2)), dma((RING, 2)), dma((RING, 2)),
            dma((PLANE,)), dma((PLANE,)),
        ],
        compiler_params=pltpu.CompilerParams(
            collective_id=0, has_side_effects=True, vmem_limit_bytes=60 << 20
        ),
        name="exchange",
    )(symmetry, wm, wr, am, d_table, e_table)


def unpack_kernel(o_ref, out_ref):
    lane = lax.broadcasted_iota(jnp.int32, (24, LANES), 1)
    cut = 12 * LANES

    def joined(v):
        middle = jnp.where(lane[: v.shape[0]] < PAD, v[:, cut:WIN], v[:, WIN : WIN + LANES])
        return v[:, :cut], middle, v[:, WIN + LANES :]

    for i in range(HALF):
        v = o_ref[3 * i : 3 * i + 3].astype(F32).reshape(24, 2 * WIN)
        start, middle, end = joined(v)
        out_ref[i, 0:24, 0:cut] = start.astype(BF16)
        out_ref[i, 0:24, cut:WIN] = middle.astype(BF16)
        out_ref[i, 0:24, WIN:] = end.astype(BF16)
        start, middle, end = joined(o_ref[24].astype(F32)[i : i + 1])
        out_ref[i, 24:25, 0:cut] = start.astype(BF16)
        out_ref[i, 24:25, cut:WIN] = middle.astype(BF16)
        out_ref[i, 24:25, WIN:] = end.astype(BF16)


def unpack(o):
    width = 2 * RING * COLS
    return pl.pallas_call(
        unpack_kernel,
        grid=(PLANE // 2,),
        out_shape=jax.ShapeDtypeStruct((HALF, ROWS, width * PLANE // 2), BF16),
        in_specs=[pl.BlockSpec((25, 8, 2 * WIN), lambda n: (0, 0, n))],
        out_specs=pl.BlockSpec((HALF, ROWS, width), lambda n: (0, 0, n)),
        compiler_params=pltpu.CompilerParams(vmem_limit_bytes=40 << 20),
        name="unpack",
    )(o)


def per_device(
    amplitudes, intermediate, occ_irrep, i_window, j_window, k_window, occ_energy, virt_energy
):
    r = lax.axis_index("rep")
    col = lax.axis_index("tensor")
    q = col // RING
    sym_k = occ_irrep[k_window]
    own_i = lax.dynamic_slice_in_dim(i_window, r * HALF, HALF)
    own_j = lax.dynamic_slice_in_dim(j_window, q * 2 * RING, 2 * RING)
    sym_i, sym_j = occ_irrep[own_i], occ_irrep[own_j]
    wm, wr, am = pack(
        lax.dynamic_slice_in_dim(sym_k, 2 * r, 2), intermediate.reshape(COLS, -1), amplitudes
    )
    irreps = jnp.arange(IRREPS, dtype=jnp.int32)
    table = virt_energy.reshape(IRREPS, VH)
    label = irreps[:, None, None] ^ sym_i[None, :, None] ^ sym_j[None, None, :]
    energy_b = jnp.zeros(label.shape + (VH,), F32)
    for value in range(IRREPS):
        energy_b = jnp.where(label[..., None] == value, table[value], energy_b)
    d_table = occ_energy[own_i][None, :, None, None] + occ_energy[own_j][None, None, :, None] - energy_b
    d_table = d_table.reshape(IRREPS, HALF, RING * COLS)
    ones = jnp.ones((IRREPS, HALF, PAD), F32)
    d_table = jnp.where(
        q % 2 == 0,
        jnp.concatenate([d_table, ones], axis=2),
        jnp.concatenate([ones, d_table], axis=2),
    )
    pairs = lax.dynamic_index_in_dim(virt_energy.reshape(IRREPS, 2, RING, ROWS), col % RING, 2, keepdims=False)
    e_rows = jnp.concatenate(
        [
            pairs[:, 0, :24], pairs[:, 1, :24],
            jnp.broadcast_to(pairs[:, 0, 24:], (IRREPS, 8)),
            jnp.broadcast_to(pairs[:, 1, 24:], (IRREPS, 8)),
        ],
        axis=1,
    )
    e_table = jnp.broadcast_to(e_rows[:, :, None], (IRREPS, BLOCK, LANES))
    o = exchange(jnp.concatenate([sym_i, sym_k]), wm, wr, am, d_table, e_table)
    return unpack(o)


def solution(mesh):
    return jax.shard_map(
        per_device,
        mesh=mesh,
        in_specs=(P("rep", "tensor", None), P("tensor", None, "rep"), P(), P(), P(), P(), P(), P()),
        out_specs=P("rep", "tensor", None),
        check_vma=False,
    )
```

time: 851 us -> 290 us (0.34)
  local copies, waits for them, and re-layouts: 641 us -> 38.3 us
  Pallas kernels: 0 us -> 245 us
  waiting for transfers between devices: 73.5 us -> 0 us
  matrix products: 50.6 us -> 0 us
  other arithmetic: 52.4 us -> 5.37 us
  between operations: 14.6 us -> 0.19 us
  starting transfers between devices: 10.5 us -> 0 us
    pallas_call x0 -> x3, Pallas kernels: none -> 245 us  [the longest x1 236 us: exchange(): pl.pallas_call(main_kernel, out_shape=jax.ShapeDtypeStruct((25, 8, PLANE...]
    broadcast_in_dim x32 -> x35, local copies, waits for them, and re-layouts: 234 us -> 9.98 us  [the longest x32 9.02 us: per_device(): energy_b = jnp.where(label[..., None] == value, table[value], energy_b)]
    unnamed x89 -> x13, local copies, waits for them, and re-layouts: 144 us -> 7.85 us
    dot_general x16 -> x0, matrix products: 50.6 us -> none  [block_product(): jnp.einsum('bwk,bkn->bwn', padded.reshape(blocks, width, depth), rights,...]
    gather x23 -> x5, local copies, waits for them, and re-layouts: 54.1 us -> 4.59 us  [the longest x1 1.33 us: per_device(): occ_energy[own_i][None, :, None, None]]
    slice x3 -> x2, local copies, waits for them, and re-layouts: 47.9 us -> 1.19 us  [the longest x1 0.98 us: per_device(): energy_b = jnp.where(label[..., None] == value, table[value], energy_b)]
    convert_element_type x2 -> x0, local copies, waits for them, and re-layouts: 41.4 us -> none  [per_device(): result = (shaped.astype(jnp.float32) / denominator).astype(jnp.bfloat16)]
    convert_element_type x2 -> x0, other arithmetic: 40.2 us -> none  [per_device(): result = (shaped.astype(jnp.float32) / denominator).astype(jnp.bfloat16)]
  transfers between devices with their start and end apart: 3 -> 0, of which waited for: 2 -> 0; matrix products, arithmetic and copies ran while one was open for 42% -> 0% of each run, Pallas kernels for 0% -> 0%
where the time goes in v1:
time: 290 us; the launch traced here: 289 us
  Pallas kernels  245 us (84%)
  local copies, waits for them, and re-layouts  38.3 us (13%)
  other arithmetic  5.37 us (2%)
    pallas_call x1, Pallas kernels, exchange(): pl.pallas_call(main_kernel, out_shape=jax.ShapeDtypeStruct((25, 8, PLANE...  236 us
    pallas_call x1, local copies, waits for them, and re-layouts, unpack(): pl.pallas_call(unpack_kernel, grid=(PLANE // 2,), out_shape=jax.ShapeDtyp...  13 us
    broadcast_in_dim x32, local copies, waits for them, and re-layouts, per_device(): energy_b = jnp.where(label[..., None] == value, table[value], energy_b)  9.02 us
    unnamed x13, local copies, waits for them, and re-layouts  7.85 us
    pallas_call x1, Pallas kernels, unpack(): pl.pallas_call(unpack_kernel, grid=(PLANE // 2,), out_shape=jax.ShapeDtyp...  6.3 us

profile of v1, /device:TPU:1, one launch (start us, length us, event | category | flops | bytes accessed | tf_op | source)
XLA Modules:
  0.0 289.0 jit_solution(7712033351906287869)
XLA Ops:
  0.0 0.9 compare_select_fusion
  0.9 0.7 compare_select_fusion.2
  1.6 0.7 compare_select_fusion.1
  2.3 0.6 gather_fusion
  2.9 1.3 gather_fusion.2
  4.3 0.6 gather_fusion.4
  4.9 1.3 gather_fusion.3
  6.3 0.6 gather_fusion.1
  7.0 0.6 pad_add_fusion.s_ref
  7.6 1.0 fusion
  8.6 0.7 broadcast_in_dim.170
  9.3 0.7 broadcast_in_dim.200
  10.0 0.7 broadcast_in_dim.195
  10.7 0.7 broadcast_in_dim.190
  11.3 0.7 broadcast_in_dim.185
  12.0 0.7 broadcast_in_dim.180
  12.7 0.7 broadcast_in_dim.175
  13.4 0.7 broadcast_in_dim.205
  14.1 0.8 reshape.119
  15.6 0.7 sub.19
  19.9 1.3 select_subtract_fusion
  21.2 1.0 pad_select_fusion.d_ref
  22.2 0.8 broadcast_in_dim.212.e_ref
  23.0 1.0 copy.18.a_ref
  24.0 3.2 %pack.1 = (bf16[8,400,384]{2,1,0:T(8,128)(2,1)S(1)}, bf16[400,128]{1,0:T(8,128)(2,1)S(1)}, bf16[2,79,8,128]{3,2,1,0:T(8,128)(2,1)S(1)}) custom-call(s32[2]{0:T(128)S(1)} %dynamic_slice.14.sk_ref, bf16[400,3200]{1,0:T(8,128)(2,1)S(1)} %bitcast.24, bf16[2,25,3200]{2,1,0:T(8,128)(2,1)S(1)} %copy.18.a_ref), custom_call_target="tpu_custom_call" | custom-call | tf_op jit(solution)/shard_map/pack/pallas_call | solution.py:64
  27.2 1.4 copy-done.3
  28.6 0.7 copy-done.4
  29.4 0.6 copy-done.5
  30.0 235.7 %exchange.1.o_ref = bf16[25,8,26624]{2,1,0:T(8,128)(2,1)} custom-call(s32[12]{0:T(128)} %pad_add_fusion.s_ref, bf16[8,400,384]{2,1,0:T(8,128)(2,1)} %copy-done.3, bf16[400,128]{1,0:T(8,128)(2,1)} %copy-done.5, bf16[2,79,8,128]{3,2,1,0:T(8,128)(2,1)} %copy-done.4, f32[8,8,1664]{2,1,0:T(8,128)} %pad_select_fusion.d_ref, f32[8,64,128]{2,1,0:T(8,128)} %broadcast_in_dim.212.e_ref), custom_call_target="tpu_custom_call" | custom-call | tf_op jit(solution)/shard_map/exchange/pallas_call | solution.py:341
  265.7 4.0 %copy-done.1 = bf16[25,8,26624]{2,1,0:T(8,128)(2,1)S(1)} copy-done((bf16[25,8,26624]{2,1,0:T(8,128)(2,1)S(1)}, bf16[25,8,26624]{2,1,0:T(8,128)(2,1)}, u32[]{:S(2)}) %copy-start.1) | copy-done | bytes 10649624
  269.7 6.3 %unpack.1 = bf16[8,25,25600]{2,1,0:T(8,128)(2,1)} custom-call(bf16[25,8,26624]{2,1,0:T(8,128)(2,1)S(1)} %copy-done.1), custom_call_target="tpu_custom_call" | custom-call | tf_op jit(solution)/shard_map/unpack/pallas_call | solution.py:386
  276.0 13.0 %copy.20 = bf16[8,25,25600]{2,0,1:T(8,128)(2,1)} copy(bf16[8,25,25600]{2,1,0:T(8,128)(2,1)} %unpack.1) | data formatting | bytes 20480000 | tf_op jit(solution)/shard_map/unpack/pallas_call | solution.py:386
  (47 shorter events, 4.4 us)
Async XLA Ops:
  0.0 2.3 copy-start
  0.0 24.0 %copy-start.2 = (bf16[2,200,3200]{2,1,0:T(8,128)(2,1)S(1)}, bf16[2,200,3200]{2,1,0:T(8,128)(2,1)}, u32[]{:S(2)}) copy-start(bf16[2,200,3200]{2,1,0:T(8,128)(2,1)} %param.9) | copy-start | bytes 7680004
  27.2 1.4 copy-start.3
  28.6 0.7 copy-start.4
  29.4 0.6 copy-start.5
  265.7 4.0 %copy-start.1 = (bf16[25,8,26624]{2,1,0:T(8,128)(2,1)S(1)}, bf16[25,8,26624]{2,1,0:T(8,128)(2,1)}, u32[]{:S(2)}) copy-start(bf16[25,8,26624]{2,1,0:T(8,128)(2,1)} %exchange.1.o_ref) | copy-start | bytes 31948804

commit v2 on v1

v2 whole, which is shorter than its diff:
```python
import functools
import jax
import jax.numpy as jnp
from jax import lax
from jax.experimental import pallas as pl
from jax.experimental.pallas import tpu as pltpu
from jax.sharding import PartitionSpec as P

IRREPS = 8
VH = 200
ROWS = 25
HALF = 8
PLANE = 16
RING = 4
COLS = 400
LANES = 128
MAIN = 384
TILES = 13
WIN = TILES * LANES
PIECES = 79
PAD = 64
BLOCK = 64
MESH = pl.DeviceIdType.MESH
F32 = jnp.float32
BF16 = jnp.bfloat16
ORDER = (
    (0, 1, 2, 3, 4, 5, 10, 11, 12, 6, 7, 8, 9),
    (4, 5, 0, 1, 2, 3, 6, 7, 8, 9, 10, 11, 12),
    (7, 8, 4, 5, 6, 9, 10, 11, 12, 0, 1, 2, 3),
    (10, 11, 12, 7, 8, 9, 0, 1, 2, 3, 4, 5, 6),
)


def pack_kernel(
    irrep_ref, k_ref, w_ref, a_ref, wm_ref, wr_ref, am_ref, wm, wr, am, rows, last, rest, sem
):
    r = lax.axis_index("rep")
    for k in range(2):
        label = irrep_ref[k_ref[2 * r + k]]
        for h in range(IRREPS):
            first = (k * IRREPS + h) * VH
            g = jnp.bitwise_xor(label, h)
            if k == 0:
                wm[g, :, 0:VH] = w_ref[:, first : first + VH]
            else:
                wm[g, :, VH:MAIN] = w_ref[:, first : first + MAIN - VH]
                wr[:, h * 16 : (h + 1) * 16] = w_ref[:, first + MAIN - VH : first + VH]
    copies = [
        pltpu.make_async_copy(wm, wm_ref, sem.at[0]),
        pltpu.make_async_copy(wr, wr_ref, sem.at[1]),
        pltpu.make_async_copy(am, am_ref, sem.at[2]),
    ]
    copies[0].start()
    copies[1].start()
    for half in range(2):
        rest[...] = jnp.zeros_like(rest)
        for i in range(HALF):
            first = (half * HALF + i) * VH
            rows[0:ROWS, 0:VH] = a_ref[0, :, first : first + VH].astype(F32)
            rows[0:ROWS, VH:COLS] = a_ref[1, :, first : first + VH].astype(F32)
            for lt in range(3):
                lanes = slice(lt * LANES, (lt + 1) * LANES)
                am[half, lt * 25 + 3 * i : lt * 25 + 3 * i + 3] = (
                    rows[0:24, lanes].reshape(3, 8, LANES).astype(BF16)
                )
                last[lt, i : i + 1, :] = rows[24:25, lanes]
            rest[0:ROWS, i * 16 : (i + 1) * 16] = rows[0:ROWS, MAIN:COLS]
        for lt in range(3):
            am[half, lt * 25 + 24] = last[lt].astype(BF16)
        am[half, 75:79] = rest[...].reshape(4, 8, LANES).astype(BF16)
    copies[2].start()
    for c in copies:
        c.wait()


def pack(irrep, k, w, a):
    vm = pl.BlockSpec(memory_space=pltpu.VMEM)
    sm = pl.BlockSpec(memory_space=pltpu.SMEM)
    hbm = pl.BlockSpec(memory_space=pl.ANY)
    shapes = ((IRREPS, COLS, MAIN), (COLS, LANES), (2, PIECES, 8, LANES))
    return pl.pallas_call(
        pack_kernel,
        out_shape=tuple(jax.ShapeDtypeStruct(shape, BF16) for shape in shapes),
        in_specs=[sm, sm, vm, vm],
        out_specs=(hbm, hbm, hbm),
        scratch_shapes=[
            *(pltpu.VMEM(shape, BF16) for shape in shapes),
            pltpu.VMEM((32, 512), F32),
            pltpu.VMEM((3, 8, LANES), F32),
            pltpu.VMEM((32, LANES), F32),
            pltpu.SemaphoreType.DMA((3,)),
        ],
        compiler_params=pltpu.CompilerParams(vmem_limit_bytes=58 << 20),
        name="pack",
    )(irrep, k, w, a)


def is_value(y, value):
    return 1 - lax.div(lax.rem(y - value + RING, RING) + RING - 1, RING)


def main_kernel(
    irrep_ref, i_ref, j_ref, k_ref, occ_ref, virt_ref, table_ref, wm_ref, wr_ref, am_ref, o_ref,
    wb, wrb, ab, left, acc, snd, dtab,
    sib_send, sib_recv, own_sem, a_send, a_recv,
    w_send, w_recv, h_send, h_recv, f_send, f_recv, o_send, o_recv,
):
    r = lax.axis_index("rep")
    col = lax.axis_index("tensor")
    q = lax.div(col, RING)
    y = lax.rem(col, RING)
    x, z = lax.div(q, 4), lax.rem(q, 4)
    phase = PAD * lax.rem(q, 2)
    sib = (1 - r, col)

    def plane_peer(o):
        px, pz = lax.rem(x + lax.div(o, 4), 4), lax.rem(z + lax.rem(o, 4), 4)
        return px * 4 + pz

    def ring_peer(d):
        return (r, q * RING + lax.rem(y + d, RING))

    barrier = pltpu.get_barrier_semaphore()

    def greet(o, c):
        pl.semaphore_signal(barrier, inc=1, device_id=(r, plane_peer(o) * RING + y), device_id_type=MESH)
        return c

    lax.fori_loop(1, PLANE, greet, 0)
    for d in (1, 3):
        pl.semaphore_signal(barrier, inc=1, device_id=ring_peer(d), device_id_type=MESH)
    pl.semaphore_signal(barrier, inc=1, device_id=sib, device_id_type=MESH)
    pl.semaphore_wait(barrier, PLANE - 1 + 2 + 1)

    def remote(src, dst, ss, rs, dev):
        return pltpu.make_async_remote_copy(
            src_ref=src, dst_ref=dst, send_sem=ss, recv_sem=rs, device_id=dev, device_id_type=MESH
        )

    def w_rows(d):
        first = PAD + COLS * lax.rem(y + RING - d, RING)
        return pl.ds(pl.multiple_of(first, 16), COLS)

    def spot(d, half):
        lanes = pl.ds(pl.multiple_of(MAIN * half, LANES), MAIN)
        rest = pl.ds(pl.multiple_of(LANES * half, LANES), LANES)
        return wb.at[:, w_rows(d), lanes], wrb.at[w_rows(d), rest]

    def w_copies(d):
        dst, dst_r = spot(0, r)
        return (
            remote(wm_ref, dst, w_send.at[d, 0], w_recv.at[d, 0], ring_peer(d)),
            remote(wr_ref, dst_r, w_send.at[d, 1], w_recv.at[d, 1], ring_peer(d)),
        )

    def w_arrivals(d):
        dst, dst_r = spot(d, r)
        return (
            remote(wm_ref, dst, w_send.at[d, 0], w_recv.at[d, 0], ring_peer(d)),
            remote(wr_ref, dst_r, w_send.at[d, 1], w_recv.at[d, 1], ring_peer(d)),
        )

    def forwards(d, half):
        dst, dst_r = spot(d, half)
        src, src_r = (wm_ref, wr_ref) if d == 0 else (dst, dst_r)
        return (
            remote(src, dst, f_send.at[d, 0], f_recv.at[d, 0], sib),
            remote(src_r, dst_r, f_send.at[d, 1], f_recv.at[d, 1], sib),
        )

    def far_copies():
        out = []
        for n, (came, to) in enumerate(((1, 1), (3, 3))):
            blocks = slice(4 * n, 4 * n + 4)
            lanes = pl.ds(pl.multiple_of(MAIN * r, LANES), MAIN)
            part = wb.at[blocks, w_rows(came), lanes]
            out.append(remote(part, part, h_send.at[n], h_recv.at[n], ring_peer(to)))
        part = wrb.at[w_rows(1), pl.ds(pl.multiple_of(LANES * r, LANES), LANES)]
        out.append(remote(part, part, h_send.at[2], h_recv.at[2], ring_peer(1)))
        return out

    def far_arrivals():
        out = []
        for n in range(2):
            lanes = pl.ds(pl.multiple_of(MAIN * r, LANES), MAIN)
            part = wb.at[4 * n : 4 * n + 4, w_rows(2), lanes]
            out.append(remote(part, part, h_send.at[n], h_recv.at[n], sib))
        part = wrb.at[w_rows(2), pl.ds(pl.multiple_of(LANES * r, LANES), LANES)]
        out.append(remote(part, part, h_send.at[2], h_recv.at[2], sib))
        return out

    a_sib = remote(am_ref.at[1 - r], ab.at[x, z, r], sib_send, sib_recv, sib)
    a_sib.start()
    a_own = pltpu.make_async_copy(am_ref.at[r], ab.at[x, z, r], own_sem.at[0])
    a_own.start()
    for d in (1, 3):
        for c in w_copies(d):
            c.start()
    for c in forwards(0, r):
        c.start()
    own_w, own_wr = spot(0, r)
    w_own = pltpu.make_async_copy(wm_ref, own_w, own_sem.at[1])
    w_own.start()
    wr_own = pltpu.make_async_copy(wr_ref, own_wr, own_sem.at[2])
    wr_own.start()
    a_own.wait()
    remote(am_ref.at[r], ab.at[x, z, 1 - r], sib_send, sib_recv, sib).wait_recv()

    def x_peer(d):
        return (r, (lax.rem(x + d, 4) * 4 + z) * RING + y)

    def z_peer(d):
        return (r, (x * 4 + lax.rem(z + d, 4)) * RING + y)

    def a_first(n, d, back):
        sx, sz = lax.rem(x + 4 - back, 4), lax.rem(z + 4 - back, 4)
        part = ab.at[sx, z, 0] if n == 0 else ab.at[x, sz, 1]
        return remote(part, part, a_send.at[0, n, d], a_recv.at[0, n, d], x_peer(d) if n == 0 else z_peer(d))

    def a_second(n, d, back):
        sx, sz = lax.rem(x + 4 - back, 4), lax.rem(z + 4 - back, 4)
        part = ab.at[:, sz, 0] if n == 0 else ab.at[sx, :, 1]
        return remote(part, part, a_send.at[1, n, d], a_recv.at[1, n, d], z_peer(d) if n == 0 else x_peer(d))

    for d in (1, 3, 2):
        for n in range(2):
            a_first(n, d, 0).start()
    for n in range(2):
        for d in (1, 3, 2):
            a_first(n, d, d).wait_recv()
        for d in (1, 3, 2):
            a_second(n, d, 0).start()

    def energies(h, c):
        for j in range(2 * RING):
            orbital_j = j_ref[q * 2 * RING + j]
            for i in range(HALF):
                orbital_i = i_ref[r * HALF + i]
                label = jnp.bitwise_xor(jnp.bitwise_xor(h, irrep_ref[orbital_i]), irrep_ref[orbital_j])
                energy = occ_ref[orbital_i] + occ_ref[orbital_j]
                dtab[h, i : i + 1, j * VH : (j + 1) * VH] = energy - table_ref[label]
        dtab[h, :, RING * COLS :] = jnp.ones((HALF, PAD), F32)
        dtab[h] = pltpu.roll(dtab[h], phase, 1)
        return c

    lax.fori_loop(0, IRREPS, energies, 0)
    for n in range(2):
        for d in (1, 3, 2):
            a_second(n, d, d).wait_recv()

    lane_group = lax.div(lax.broadcasted_iota(jnp.int32, (BLOCK, LANES), 1), 16)

    def build(g, c):
        for i in range(HALF):
            h = jnp.bitwise_xor(g, irrep_ref[i_ref[r * HALF + i]])
            hx, hz = lax.div(h, 2), 2 * lax.rem(h, 2)
            base = i * BLOCK
            for half in range(2):
                for lt in range(3):
                    lanes = slice(half * MAIN + lt * LANES, half * MAIN + (lt + 1) * LANES)
                    parts = [
                        ab[hx, hz + zp, half, lt * 25 + 3 * i : lt * 25 + 3 * i + 3].astype(F32).reshape(24, LANES)
                        for zp in range(2)
                    ] + [ab[hx, hz + zp, half, lt * 25 + 24].astype(F32) for zp in range(2)]
                    left[g, base : base + BLOCK, lanes] = jnp.concatenate(parts, axis=0).astype(BF16)
                tails = [ab[hx, hz + zp, half, 75:79].astype(F32).reshape(32, LANES) for zp in range(2)]
                parts = [t[0:24] for t in tails] + [jnp.broadcast_to(t[24:25], (8, LANES)) for t in tails]
                tail = jnp.concatenate(parts, axis=0)
                place = jnp.bitwise_xor(g, irrep_ref[k_ref[2 * half + 1]])
                tail = pltpu.roll(tail, lax.rem(16 * (place - i) + LANES, LANES), 1)
                tail = jnp.where(lane_group == place, tail, 0.0)
                lanes = slice(2 * MAIN + half * LANES, 2 * MAIN + (half + 1) * LANES)
                left[g, base : base + BLOCK, lanes] = tail.astype(BF16)
        return c

    lax.fori_loop(0, IRREPS, build, 0)
    w_own.wait()
    wr_own.wait()
    for c in forwards(0, 1 - r):
        c.wait_recv()

    lo, hi = 0, 0
    for value in range(RING):
        picked = is_value(y, value)
        lo = lo + picked * sum(ORDER[value][p] * 16**p for p in range(7))
        hi = hi + picked * sum(ORDER[value][p + 7] * 16**p for p in range(6))
    row_index = lax.broadcasted_iota(jnp.int32, (8, LANES), 0)
    NT = (((1,), (1,)), ((), ()))

    def out_copy(p, t, peer):
        return snd.at[p, peer], o_ref.at[q * TILES + t]

    def step(p, carry):
        lo, hi = carry
        t = lax.rem(lo, 16)

        @pl.when(p == 2)
        def _():
            for d in (1, 3):
                for c in w_arrivals(d):
                    c.wait_recv()
            for c in far_copies():
                c.start()
            for d in (1, 3):
                for c in forwards(d, r):
                    c.start()
            for d in (1, 3):
                for c in forwards(d, 1 - r):
                    c.wait_recv()

        @pl.when(p == 9)
        def _():
            for c in far_arrivals():
                c.wait_recv()
            for c in forwards(2, r):
                c.start()
            for c in forwards(2, 1 - r):
                c.wait_recv()

        window = pl.ds(pl.multiple_of(t * LANES + PAD - phase, 16), LANES)

        def multiply(g, c):
            total = lax.dot_general(
                left[g, :, 0 : 2 * MAIN], wb[g, window, :], NT, preferred_element_type=F32
            )
            total = total + lax.dot_general(
                left[g, :, 2 * MAIN :], wrb[window, :], NT, preferred_element_type=F32
            )
            acc[g] = total.reshape(HALF, BLOCK, LANES)
            return c

        lax.fori_loop(0, IRREPS, multiply, 0)
        lanes = pl.ds(pl.multiple_of(t * LANES, LANES), LANES)

        def finish(s, c):
            h = 2 * lax.rem(x + lax.div(s, 2), 4) + lax.rem(lax.div(z, 2) + s, 2)
            values = [acc[jnp.bitwise_xor(h, irrep_ref[i_ref[r * HALF + i]]), i] for i in range(HALF)]
            energy = dtab[h, :, lanes]
            for zp in range(2):
                first = ROWS * (8 * h + 4 * zp + y)
                last = jnp.zeros((8, LANES), F32)
                for i in range(HALF):
                    last = jnp.where(row_index == i, values[i][48 + 8 * zp : 56 + 8 * zp], last)
                snd[p, 2 * h + zp, 24] = (last / (energy - virt_ref[first + 24])).astype(BF16)
                for n in range(3):
                    top = 24 * zp + 8 * n
                    tiles = jnp.stack([v[top : top + 8] for v in values]).transpose(1, 0, 2)
                    for m in range(8):
                        value = tiles[m] / (energy - virt_ref[first + 8 * n + m])
                        snd[p, 2 * h + zp, 8 * n + m] = value.astype(BF16)
            for zp in range(2):
                peer = 2 * h + zp
                src, dst = out_copy(p, t, peer)

                @pl.when(peer != q)
                def _():
                    remote(src, dst, o_send.at[peer], o_recv.at[q], (r, peer * RING + y)).start()

                @pl.when(peer == q)
                def _():
                    pltpu.make_async_copy(src, dst, o_send.at[peer]).start()

            return c

        lax.fori_loop(0, IRREPS, finish, 0)
        return lax.div(lo, 16) + lax.rem(hi, 16) * 16**6, lax.div(hi, 16)

    lax.fori_loop(0, TILES, step, (lo, hi))

    a_sib.wait_send()
    for d in range(RING):
        for c in forwards(d, r):
            c.wait_send()
    for d in (1, 3):
        for c in w_copies(d):
            c.wait_send()
    for c in far_copies():
        c.wait_send()
    for n in range(2):
        for d in (1, 3, 2):
            a_first(n, d, 0).wait_send()
            a_second(n, d, 0).wait_send()

    def all_tiles(peer):
        return o_ref.at[pl.ds(peer * TILES, TILES)]

    def drain_out(o, c):
        peer = plane_peer(o)
        whole = all_tiles(peer)
        remote(whole, whole, o_send.at[peer], o_recv.at[peer], sib).wait_send()
        remote(whole, whole, o_send.at[peer], o_recv.at[peer], sib).wait_recv()
        return c

    lax.fori_loop(1, PLANE, drain_out, 0)
    own = all_tiles(q)
    pltpu.make_async_copy(own, own, o_send.at[q]).wait()


def exchange(irrep, i, j, k, occ, virt, wm, wr, am):
    vm = pl.BlockSpec(memory_space=pltpu.VMEM)
    sm = pl.BlockSpec(memory_space=pltpu.SMEM)
    hbm = pl.BlockSpec(memory_space=pl.ANY)
    dma = pltpu.SemaphoreType.DMA
    return pl.pallas_call(
        main_kernel,
        out_shape=jax.ShapeDtypeStruct((PLANE * TILES, ROWS, 8, LANES), BF16),
        in_specs=[sm, sm, sm, sm, sm, sm, vm, hbm, hbm, hbm],
        out_specs=hbm,
        scratch_shapes=[
            pltpu.VMEM((IRREPS, RING * COLS + 2 * PAD, 2 * MAIN), BF16),
            pltpu.VMEM((RING * COLS + 2 * PAD, 2 * LANES), BF16),
            pltpu.VMEM((4, 4, 2, PIECES, 8, LANES), BF16),
            pltpu.VMEM((IRREPS, HALF * BLOCK, 2 * MAIN + 2 * LANES), BF16),
            pltpu.VMEM((IRREPS, HALF, BLOCK, LANES), F32),
            pltpu.VMEM((TILES, PLANE, ROWS, 8, LANES), BF16),
            pltpu.VMEM((IRREPS, HALF, WIN), F32),
            dma, dma, dma((3,)), dma((2, 2, 4)), dma((2, 2, 4)),
            dma((RING, 2)), dma((RING, 2)), dma((3,)), dma((3,)), dma((RING, 2)), dma((RING, 2)),
            dma((PLANE,)), dma((PLANE,)),
        ],
        compiler_params=pltpu.CompilerParams(
            collective_id=0, has_side_effects=True, vmem_limit_bytes=60 << 20
        ),
        name="exchange",
    )(irrep, i, j, k, occ, virt, virt.reshape(IRREPS, 1, VH), wm, wr, am)


def unpack_kernel(o_ref, out_ref):
    low = lax.broadcasted_iota(jnp.int32, (ROWS, 8, LANES), 2) < PAD
    for t in range(TILES - 1):
        out_ref[:, :, t * LANES : (t + 1) * LANES] = o_ref[t]
        out_ref[:, :, (t + TILES) * LANES : (t + TILES + 1) * LANES] = o_ref[t + TILES + 1]
    middle = jnp.where(low, o_ref[TILES - 1].astype(F32), o_ref[TILES].astype(F32))
    out_ref[:, :, WIN - LANES : WIN] = middle.astype(BF16)


def unpack(o):
    width = 2 * RING * COLS
    return pl.pallas_call(
        unpack_kernel,
        grid=(PLANE // 2,),
        out_shape=jax.ShapeDtypeStruct((ROWS, HALF, width * PLANE // 2), BF16),
        in_specs=[pl.BlockSpec((2 * TILES, ROWS, 8, LANES), lambda n: (n, 0, 0, 0))],
        out_specs=pl.BlockSpec((ROWS, HALF, width), lambda n: (0, 0, n)),
        compiler_params=pltpu.CompilerParams(vmem_limit_bytes=58 << 20),
        name="unpack",
    )(o)


def per_device(
    amplitudes, intermediate, occ_irrep, i_window, j_window, k_window, occ_energy, virt_energy
):
    wm, wr, am = pack(occ_irrep, k_window, intermediate.reshape(COLS, -1), amplitudes)
    o = exchange(
        occ_irrep, i_window, j_window, k_window, occ_energy, virt_energy, wm, wr, am
    )
    return unpack(o).transpose(1, 0, 2)


def solution(mesh):
    return jax.shard_map(
        per_device,
        mesh=mesh,
        in_specs=(P("rep", "tensor", None), P("tensor", None, "rep"), P(), P(), P(), P(), P(), P()),
        out_specs=P("rep", "tensor", None),
        check_vma=False,
    )
```

time: 290 us -> 207 us (0.71)
  the two profiles are of different devices: /device:TPU:1 before, /device:TPU:35 now
where the time goes in v2:
time: 207 us; the launch traced here: 206 us
  Pallas kernels  203 us (98%)
  local copies, waits for them, and re-layouts  3.14 us (2%)
    pallas_call x1, Pallas kernels, exchange(): pl.pallas_call(main_kernel, out_shape=jax.ShapeDtypeStruct((PLANE * TILES...  187 us
    pallas_call x1, Pallas kernels, unpack(): pl.pallas_call(unpack_kernel, grid=(PLANE // 2,), out_shape=jax.ShapeDtyp...  10.6 us
    pallas_call x1, Pallas kernels, pack(): pl.pallas_call(pack_kernel, out_shape=tuple((jax.ShapeDtypeStruct(shape,...  5.2 us

profile of v2, /device:TPU:35, one launch (start us, length us, event | category | flops | bytes accessed | tf_op | source)
XLA Modules:
  0.0 206.1 jit_solution(1502578965069977205)
XLA Ops:
  0.0 1.4 reshape.6.table_ref
  1.4 1.8 copy.9.a_ref
  3.1 5.2 %pack.1 = (bf16[8,400,384]{2,1,0:T(8,128)(2,1)}, bf16[400,128]{1,0:T(8,128)(2,1)}, bf16[2,79,8,128]{3,2,1,0:T(8,128)(2,1)}) custom-call(s32[200]{0:T(256)} %irrep_ref.3, s32[4]{0:T(128)} %k_ref.3, bf16[400,3200]{1,0:T(8,128)(2,1)} %bitcast.2, bf16[2,25,3200]{2,1,0:T(8,128)(2,1)} %copy.9.a_ref), custom_call_target="tpu_custom_call" | custom-call | tf_op jit(solution)/shard_map/pack/pallas_call | solution.py:81
  8.4 187.1 %exchange.1.o_ref = bf16[208,25,8,128]{3,2,1,0:T(8,128)(2,1)} custom-call(s32[200]{0:T(256)} %irrep_ref.3, s32[16]{0:T(128)} %i_ref.1, s32[128]{0:T(128)} %j_ref.1, s32[4]{0:T(128)} %k_ref.3, f32[200]{0:T(256)} %occ_ref.1, f32[1600]{0:T(1024)} %virt_ref.1, f32[8,1,200]{2,1,0:T(1,128)} %reshape.6.table_ref, bf16[8,400,384]{2,1,0:T(8,128)(2,1)} %get-tuple-element.8.wm_ref, ...), custom_call_target="tpu_custom_call" | custom-call | tf_op jit(solution)/shard_map/exchange/pallas_call | solution.py:404
  195.5 10.6 %unpack.1 = bf16[25,8,25600]{2,1,0:T(8,128)(2,1)} custom-call(bf16[208,25,8,128]{3,2,1,0:T(8,128)(2,1)} %exchange.1.o_ref), custom_call_target="tpu_custom_call" | custom-call | tf_op jit(solution)/shard_map/unpack/pallas_call | solution.py:439

commit v3 on v2

--- a/solution.py
+++ b/solution.py
@@ -24,10 +24,15 @@
 F32 = jnp.float32
 BF16 = jnp.bfloat16
 ORDER = (
-    (0, 1, 2, 3, 4, 5, 10, 11, 12, 6, 7, 8, 9),
-    (4, 5, 0, 1, 2, 3, 6, 7, 8, 9, 10, 11, 12),
-    (7, 8, 4, 5, 6, 9, 10, 11, 12, 0, 1, 2, 3),
-    (10, 11, 12, 7, 8, 9, 0, 1, 2, 3, 4, 5, 6),
+    (0, 1, 2, 3, 4, 11, 12, 5, 10, 6, 7, 8, 9),
+    (4, 5, 3, 2, 6, 7, 0, 1, 8, 9, 10, 11, 12),
+    (7, 8, 6, 5, 9, 10, 4, 11, 12, 0, 1, 2, 3),
+    (10, 11, 12, 9, 8, 0, 1, 7, 2, 3, 4, 5, 6),
+)
+PARTS = {1: ((144, 256), (0, 144)), 3: ((0, 256), (256, 144))}
+SENDS = (
+    (2, 2), (2, 1), (1, 2), (2, 3), (3, 2), (1, 1), (3, 3), (1, 3),
+    (3, 1), (2, 0), (0, 2), (1, 0), (0, 1), (3, 0), (0, 3),
 )
 
 
@@ -137,65 +142,55 @@
             src_ref=src, dst_ref=dst, send_sem=ss, recv_sem=rs, device_id=dev, device_id_type=MESH
         )
 
-    def w_rows(d):
-        first = PAD + COLS * lax.rem(y + RING - d, RING)
-        return pl.ds(pl.multiple_of(first, 16), COLS)
-
-    def spot(d, half):
+    def spot(back, half, first=0, size=COLS):
+        top = PAD + COLS * lax.rem(y + RING - back, RING) + first
+        rows = pl.ds(pl.multiple_of(top, 16), size)
         lanes = pl.ds(pl.multiple_of(MAIN * half, LANES), MAIN)
         rest = pl.ds(pl.multiple_of(LANES * half, LANES), LANES)
-        return wb.at[:, w_rows(d), lanes], wrb.at[w_rows(d), rest]
-
-    def w_copies(d):
-        dst, dst_r = spot(0, r)
+        return wb.at[:, rows, lanes], wrb.at[rows, rest]
+
+    def w_copies(d, part, back):
+        first, size = PARTS[d][part]
+        rows = pl.ds(first, size)
+        dst, dst_r = spot(back, r, first, size)
         return (
-            remote(wm_ref, dst, w_send.at[d, 0], w_recv.at[d, 0], ring_peer(d)),
-            remote(wr_ref, dst_r, w_send.at[d, 1], w_recv.at[d, 1], ring_peer(d)),
+            remote(wm_ref.at[:, rows], dst, w_send.at[d, part, 0], w_recv.at[d, part, 0], ring_peer(d)),
+            remote(wr_ref.at[rows], dst_r, w_send.at[d, part, 1], w_recv.at[d, part, 1], ring_peer(d)),
         )
 
-    def w_arrivals(d):
-        dst, dst_r = spot(d, r)
-        return (
-            remote(wm_ref, dst, w_send.at[d, 0], w_recv.at[d, 0], ring_peer(d)),
-            remote(wr_ref, dst_r, w_send.at[d, 1], w_recv.at[d, 1], ring_peer(d)),
-        )
-
-    def forwards(d, half):
-        dst, dst_r = spot(d, half)
+    def forwards(d, half, part=0):
+        first, size = PARTS[d][part] if d in PARTS else (0, COLS)
+        dst, dst_r = spot(d, half, first, size)
         src, src_r = (wm_ref, wr_ref) if d == 0 else (dst, dst_r)
         return (
-            remote(src, dst, f_send.at[d, 0], f_recv.at[d, 0], sib),
-            remote(src_r, dst_r, f_send.at[d, 1], f_recv.at[d, 1], sib),
+            remote(src, dst, f_send.at[d, part, 0], f_recv.at[d, part, 0], sib),
+            remote(src_r, dst_r, f_send.at[d, part, 1], f_recv.at[d, part, 1], sib),
         )
 
+    def far(back):
+        out = []
+        for n, d in enumerate((1, 3)):
+            main, rest = spot(d if back is None else back, r)
+            part = main.at[4 * n : 4 * n + 4]
+            out.append(remote(part, part, h_send.at[n], h_recv.at[n], ring_peer(d)))
+            if n == 0:
+                out.append(remote(rest, rest, h_send.at[2], h_recv.at[2], ring_peer(d)))
+        return out
+
     def far_copies():
-        out = []
-        for n, (came, to) in enumerate(((1, 1), (3, 3))):
-            blocks = slice(4 * n, 4 * n + 4)
-            lanes = pl.ds(pl.multiple_of(MAIN * r, LANES), MAIN)
-            part = wb.at[blocks, w_rows(came), lanes]
-            out.append(remote(part, part, h_send.at[n], h_recv.at[n], ring_peer(to)))
-        part = wrb.at[w_rows(1), pl.ds(pl.multiple_of(LANES * r, LANES), LANES)]
-        out.append(remote(part, part, h_send.at[2], h_recv.at[2], ring_peer(1)))
-        return out
+        return far(None)
 
     def far_arrivals():
-        out = []
-        for n in range(2):
-            lanes = pl.ds(pl.multiple_of(MAIN * r, LANES), MAIN)
-            part = wb.at[4 * n : 4 * n + 4, w_rows(2), lanes]
-            out.append(remote(part, part, h_send.at[n], h_recv.at[n], sib))
-        part = wrb.at[w_rows(2), pl.ds(pl.multiple_of(LANES * r, LANES), LANES)]
-        out.append(remote(part, part, h_send.at[2], h_recv.at[2], sib))
-        return out
+        return far(2)
 
     a_sib = remote(am_ref.at[1 - r], ab.at[x, z, r], sib_send, sib_recv, sib)
     a_sib.start()
     a_own = pltpu.make_async_copy(am_ref.at[r], ab.at[x, z, r], own_sem.at[0])
     a_own.start()
-    for d in (1, 3):
-        for c in w_copies(d):
-            c.start()
+    for part in range(2):
+        for d in (1, 3):
+            for c in w_copies(d, part, 0):
+                c.start()
     for c in forwards(0, r):
         c.start()
     own_w, own_wr = spot(0, r)
@@ -212,15 +207,24 @@
     def z_peer(d):
         return (r, (x * 4 + lax.rem(z + d, 4)) * RING + y)
 
+    def a_peer(n, d):
+        return x_peer(d) if n == 0 else z_peer(d)
+
     def a_first(n, d, back):
         sx, sz = lax.rem(x + 4 - back, 4), lax.rem(z + 4 - back, 4)
         part = ab.at[sx, z, 0] if n == 0 else ab.at[x, sz, 1]
-        return remote(part, part, a_send.at[0, n, d], a_recv.at[0, n, d], x_peer(d) if n == 0 else z_peer(d))
+        return remote(part, part, a_send.at[0, n, d], a_recv.at[0, n, d], a_peer(n, d))
 
     def a_second(n, d, back):
         sx, sz = lax.rem(x + 4 - back, 4), lax.rem(z + 4 - back, 4)
         part = ab.at[:, sz, 0] if n == 0 else ab.at[sx, :, 1]
-        return remote(part, part, a_send.at[1, n, d], a_recv.at[1, n, d], z_peer(d) if n == 0 else x_peer(d))
+        return remote(part, part, a_send.at[1, n, d], a_recv.at[1, n, d], a_peer(1 - n, d))
+
+    def a_third(n, d, back):
+        sx, sz = lax.rem(x + 4 - back, 4), lax.rem(z + 4 - back, 4)
+        pick = slice(0, 2) if d == 1 else slice(2, 4)
+        part = ab.at[pick, sz, 0] if n == 0 else ab.at[sx, pick, 1]
+        return remote(part, part, a_send.at[2, n, d], a_recv.at[2, n, d], a_peer(1 - n, d))
 
     for d in (1, 3, 2):
         for n in range(2):
@@ -228,7 +232,7 @@
     for n in range(2):
         for d in (1, 3, 2):
             a_first(n, d, d).wait_recv()
-        for d in (1, 3, 2):
+        for d in (1, 3):
             a_second(n, d, 0).start()
 
     def energies(h, c):
@@ -245,8 +249,12 @@
 
     lax.fori_loop(0, IRREPS, energies, 0)
     for n in range(2):
-        for d in (1, 3, 2):
+        for d in (1, 3):
             a_second(n, d, d).wait_recv()
+            a_third(n, d, d).start()
+    for n in range(2):
+        for d in (1, 3):
+            a_third(n, d, 2).wait_recv()
 
     lane_group = lax.div(lax.broadcasted_iota(jnp.int32, (BLOCK, LANES), 1), 16)
 
@@ -294,19 +302,26 @@
         lo, hi = carry
         t = lax.rem(lo, 16)
 
+        def neighbours(part):
+            for d in (1, 3):
+                for c in w_copies(d, part, d):
+                    c.wait_recv()
+                for c in forwards(d, r, part):
+                    c.start()
+            if part == 1:
+                for c in far_copies():
+                    c.start()
+            for d in (1, 3):
+                for c in forwards(d, 1 - r, part):
+                    c.wait_recv()
+
         @pl.when(p == 2)
         def _():
-            for d in (1, 3):
-                for c in w_arrivals(d):
-                    c.wait_recv()
-            for c in far_copies():
-                c.start()
-            for d in (1, 3):
-                for c in forwards(d, r):
-                    c.start()
-            for d in (1, 3):
-                for c in forwards(d, 1 - r):
-                    c.wait_recv()
+            neighbours(0)
+
+        @pl.when(p == 6)
+        def _():
+            neighbours(1)
 
         @pl.when(p == 9)
         def _():
@@ -348,38 +363,35 @@
                     for m in range(8):
                         value = tiles[m] / (energy - virt_ref[first + 8 * n + m])
                         snd[p, 2 * h + zp, 8 * n + m] = value.astype(BF16)
-            for zp in range(2):
-                peer = 2 * h + zp
-                src, dst = out_copy(p, t, peer)
-
-                @pl.when(peer != q)
-                def _():
-                    remote(src, dst, o_send.at[peer], o_recv.at[q], (r, peer * RING + y)).start()
-
-                @pl.when(peer == q)
-                def _():
-                    pltpu.make_async_copy(src, dst, o_send.at[peer]).start()
-
             return c
 
         lax.fori_loop(0, IRREPS, finish, 0)
+        for ox, oz in SENDS:
+            peer = lax.rem(x + ox, 4) * 4 + lax.rem(z + oz, 4)
+            src, dst = out_copy(p, t, peer)
+            remote(src, dst, o_send.at[peer], o_recv.at[q], (r, peer * RING + y)).start()
+        src, dst = out_copy(p, t, q)
+        pltpu.make_async_copy(src, dst, o_send.at[q]).start()
         return lax.div(lo, 16) + lax.rem(hi, 16) * 16**6, lax.div(hi, 16)
 
     lax.fori_loop(0, TILES, step, (lo, hi))
 
     a_sib.wait_send()
-    for d in range(RING):
+    for d in (0, 2):
         for c in forwards(d, r):
             c.wait_send()
     for d in (1, 3):
-        for c in w_copies(d):
-            c.wait_send()
+        for part in range(2):
+            for c in (*forwards(d, r, part), *w_copies(d, part, 0)):
+                c.wait_send()
     for c in far_copies():
         c.wait_send()
     for n in range(2):
         for d in (1, 3, 2):
             a_first(n, d, 0).wait_send()
+        for d in (1, 3):
             a_second(n, d, 0).wait_send()
+            a_third(n, d, d).wait_send()
 
     def all_tiles(peer):
         return o_ref.at[pl.ds(peer * TILES, TILES)]
@@ -414,8 +426,8 @@
             pltpu.VMEM((IRREPS, HALF, BLOCK, LANES), F32),
             pltpu.VMEM((TILES, PLANE, ROWS, 8, LANES), BF16),
             pltpu.VMEM((IRREPS, HALF, WIN), F32),
-            dma, dma, dma((3,)), dma((2, 2, 4)), dma((2, 2, 4)),
-            dma((RING, 2)), dma((RING, 2)), dma((3,)), dma((3,)), dma((RING, 2)), dma((RING, 2)),
+            dma, dma, dma((3,)), dma((3, 2, 4)), dma((3, 2, 4)),
+            dma((RING, 2, 2)), dma((RING, 2, 2)), dma((3,)), dma((3,)), dma((RING, 2, 2)), dma((RING, 2, 2)),
             dma((PLANE,)), dma((PLANE,)),
         ],
         compiler_params=pltpu.CompilerParams(
@@ -425,23 +437,47 @@
     )(irrep, i, j, k, occ, virt, virt.reshape(IRREPS, 1, VH), wm, wr, am)
 
 
-def unpack_kernel(o_ref, out_ref):
+def unpack_kernel(o_hbm, out_ref, o_ref, middle, sem, in_sem):
     low = lax.broadcasted_iota(jnp.int32, (ROWS, 8, LANES), 2) < PAD
-    for t in range(TILES - 1):
-        out_ref[:, :, t * LANES : (t + 1) * LANES] = o_ref[t]
-        out_ref[:, :, (t + TILES) * LANES : (t + TILES + 1) * LANES] = o_ref[t + TILES + 1]
-    middle = jnp.where(low, o_ref[TILES - 1].astype(F32), o_ref[TILES].astype(F32))
-    out_ref[:, :, WIN - LANES : WIN] = middle.astype(BF16)
+
+    def place(src, tile, n):
+        lanes = pl.ds(pl.multiple_of(tile * LANES, LANES), LANES)
+        return pltpu.make_async_copy(src, out_ref.at[:, :, lanes], sem.at[n])
+
+    def load(n):
+        part = pl.ds(n * 2 * TILES, 2 * TILES)
+        return pltpu.make_async_copy(o_hbm.at[part], o_ref.at[part], in_sem.at[n])
+
+    for n in range(PLANE // 2):
+        load(n).start()
+
+    def pair(n, c):
+        load(n).wait()
+        for t in range(TILES - 1):
+            place(o_ref.at[n * 2 * TILES + t], n * 25 + t, 0).start()
+            place(o_ref.at[n * 2 * TILES + TILES + 1 + t], n * 25 + TILES + t, 0).start()
+        even = o_ref[n * 2 * TILES + TILES - 1].astype(F32)
+        odd = o_ref[n * 2 * TILES + TILES].astype(F32)
+        middle[n] = jnp.where(low, even, odd).astype(BF16)
+        place(middle.at[n], n * 25 + TILES - 1, 0).start()
+        return c
+
+    lax.fori_loop(0, PLANE // 2, pair, 0)
+    pltpu.make_async_copy(out_ref, out_ref, sem.at[0]).wait()
 
 
 def unpack(o):
-    width = 2 * RING * COLS
     return pl.pallas_call(
         unpack_kernel,
-        grid=(PLANE // 2,),
-        out_shape=jax.ShapeDtypeStruct((ROWS, HALF, width * PLANE // 2), BF16),
-        in_specs=[pl.BlockSpec((2 * TILES, ROWS, 8, LANES), lambda n: (n, 0, 0, 0))],
-        out_specs=pl.BlockSpec((ROWS, HALF, width), lambda n: (0, 0, n)),
+        out_shape=jax.ShapeDtypeStruct((ROWS, HALF, RING * COLS * PLANE), BF16),
+        in_specs=[pl.BlockSpec(memory_space=pl.ANY)],
+        out_specs=pl.BlockSpec(memory_space=pl.ANY),
+        scratch_shapes=[
+            pltpu.VMEM((PLANE * TILES, ROWS, 8, LANES), BF16),
+            pltpu.VMEM((PLANE // 2, ROWS, 8, LANES), BF16),
+            pltpu.SemaphoreType.DMA((1,)),
+            pltpu.SemaphoreType.DMA((PLANE // 2,)),
+        ],
         compiler_params=pltpu.CompilerParams(vmem_limit_bytes=58 << 20),
         name="unpack",
     )(o)

time: 207 us -> 187 us (0.903)
  the two profiles are of different devices: /device:TPU:35 before, /device:TPU:1 now
where the time goes in v3:
time: 187 us; the launch traced here: 184 us
  Pallas kernels  181 us (97%)
  local copies, waits for them, and re-layouts  3.14 us (2%)
    pallas_call x1, Pallas kernels, exchange(): pl.pallas_call(main_kernel, out_shape=jax.ShapeDtypeStruct((PLANE * TILES...  168 us
    pallas_call x1, Pallas kernels, unpack(): pl.pallas_call(unpack_kernel, out_shape=jax.ShapeDtypeStruct((ROWS, HALF,...  8.01 us
    pallas_call x1, Pallas kernels, pack(): pl.pallas_call(pack_kernel, out_shape=tuple((jax.ShapeDtypeStruct(shape,...  5.2 us

profile of v3, /device:TPU:1, one launch (start us, length us, event | category | flops | bytes accessed | tf_op | source)
XLA Modules:
  0.0 184.1 jit_solution(10087205290674078361)
XLA Ops:
  0.0 1.4 reshape.6.table_ref
  1.4 1.8 copy.9.a_ref
  3.1 5.2 %pack.1 = (bf16[8,400,384]{2,1,0:T(8,128)(2,1)}, bf16[400,128]{1,0:T(8,128)(2,1)}, bf16[2,79,8,128]{3,2,1,0:T(8,128)(2,1)}) custom-call(s32[200]{0:T(256)} %irrep_ref.3, s32[4]{0:T(128)} %k_ref.3, bf16[400,3200]{1,0:T(8,128)(2,1)} %bitcast.2, bf16[2,25,3200]{2,1,0:T(8,128)(2,1)} %copy.9.a_ref), custom_call_target="tpu_custom_call" | custom-call | tf_op jit(solution)/shard_map/pack/pallas_call | solution.py:86
  8.4 167.7 %exchange.1.o_hbm = bf16[208,25,8,128]{3,2,1,0:T(8,128)(2,1)} custom-call(s32[200]{0:T(256)} %irrep_ref.3, s32[16]{0:T(128)} %i_ref.1, s32[128]{0:T(128)} %j_ref.1, s32[4]{0:T(128)} %k_ref.3, f32[200]{0:T(256)} %occ_ref.1, f32[1600]{0:T(1024)} %virt_ref.1, f32[8,1,200]{2,1,0:T(1,128)} %reshape.6.table_ref, bf16[8,400,384]{2,1,0:T(8,128)(2,1)} %get-tuple-element.8.wm_ref, ...), custom_call_target="tpu_custom_call" | custom-call | tf_op jit(solution)/shard_map/exchange/pallas_call | solution.py:416
  176.1 8.0 %unpack.1 = bf16[25,8,25600]{2,1,0:T(8,128)(2,1)} custom-call(bf16[208,25,8,128]{3,2,1,0:T(8,128)(2,1)} %exchange.1.o_hbm), custom_call_target="tpu_custom_call" | custom-call | tf_op jit(solution)/shard_map/unpack/pallas_call | solution.py:470

commit v4 on v3

--- a/solution.py
+++ b/solution.py
@@ -16,6 +16,7 @@
 LANES = 128
 MAIN = 384
 TILES = 13
+HALVES = 13
 WIN = TILES * LANES
 PIECES = 79
 PAD = 64
@@ -24,12 +25,13 @@
 F32 = jnp.float32
 BF16 = jnp.bfloat16
 ORDER = (
-    (0, 1, 2, 3, 4, 11, 12, 5, 10, 6, 7, 8, 9),
+    (1, 2, 3, 4, 11, 0, 5, 10, 12, 6, 7, 8, 9),
     (4, 5, 3, 2, 6, 7, 0, 1, 8, 9, 10, 11, 12),
     (7, 8, 6, 5, 9, 10, 4, 11, 12, 0, 1, 2, 3),
     (10, 11, 12, 9, 8, 0, 1, 7, 2, 3, 4, 5, 6),
 )
 PARTS = {1: ((144, 256), (0, 144)), 3: ((0, 256), (256, 144))}
+THIRD = {1: (0, 3), 3: (1, 2)}
 SENDS = (
     (2, 2), (2, 1), (1, 2), (2, 3), (3, 2), (1, 1), (3, 3), (1, 3),
     (3, 1), (2, 0), (0, 2), (1, 0), (0, 1), (3, 0), (0, 3),
@@ -105,10 +107,10 @@
 
 
 def main_kernel(
-    irrep_ref, i_ref, j_ref, k_ref, occ_ref, virt_ref, table_ref, wm_ref, wr_ref, am_ref, o_ref,
-    wb, wrb, ab, left, acc, snd, dtab,
+    irrep_ref, i_ref, j_ref, k_ref, occ_ref, virt_ref, line_ref, wm_ref, wr_ref, am_ref, o_ref,
+    wb, wrb, ab, left, acc, snd, dtab, table_ref,
     sib_send, sib_recv, own_sem, a_send, a_recv,
-    w_send, w_recv, h_send, h_recv, f_send, f_recv, o_send, o_recv,
+    w_send, w_recv, h_send, h_recv, f_send, f_recv, o_send, o_recv, e_send, e_recv,
 ):
     r = lax.axis_index("rep")
     col = lax.axis_index("tensor")
@@ -199,7 +201,6 @@
     wr_own = pltpu.make_async_copy(wr_ref, own_wr, own_sem.at[2])
     wr_own.start()
     a_own.wait()
-    remote(am_ref.at[r], ab.at[x, z, 1 - r], sib_send, sib_recv, sib).wait_recv()
 
     def x_peer(d):
         return (r, (lax.rem(x + d, 4) * 4 + z) * RING + y)
@@ -215,25 +216,36 @@
         part = ab.at[sx, z, 0] if n == 0 else ab.at[x, sz, 1]
         return remote(part, part, a_send.at[0, n, d], a_recv.at[0, n, d], a_peer(n, d))
 
-    def a_second(n, d, back):
-        sx, sz = lax.rem(x + 4 - back, 4), lax.rem(z + 4 - back, 4)
-        part = ab.at[:, sz, 0] if n == 0 else ab.at[sx, :, 1]
-        return remote(part, part, a_send.at[1, n, d], a_recv.at[1, n, d], a_peer(1 - n, d))
-
-    def a_third(n, d, back):
-        sx, sz = lax.rem(x + 4 - back, 4), lax.rem(z + 4 - back, 4)
-        pick = slice(0, 2) if d == 1 else slice(2, 4)
-        part = ab.at[pick, sz, 0] if n == 0 else ab.at[sx, pick, 1]
-        return remote(part, part, a_send.at[2, n, d], a_recv.at[2, n, d], a_peer(1 - n, d))
-
+    def a_entry(n, fixed, offset):
+        sx, sz = lax.rem(x + 4 - (offset if n == 0 else fixed), 4), lax.rem(z + 4 - (fixed if n == 0 else offset), 4)
+        return ab.at[sx, sz, n]
+
+    def a_second(n, d, back, offset):
+        part = a_entry(n, back, offset)
+        return remote(part, part, a_send.at[1 + offset, n, d], a_recv.at[1 + offset, n, d], a_peer(1 - n, d))
+
+    def a_third(n, d, back, offset):
+        part = a_entry(n, back, offset)
+        return remote(part, part, a_send.at[5 + offset, n, d], a_recv.at[5 + offset, n, d], a_peer(1 - n, d))
+
+    def a_second_start(n, offset):
+        for d in (1, 3):
+            a_second(n, d, 0, offset).start()
+
+    def a_half_start(n):
+        for d in (1, 3, 2):
+            a_first(n, d, 0).start()
+        a_second_start(n, 0)
+
+    for n in range(2):
+        pl.when(r == n)(functools.partial(a_half_start, n))
+    remote(am_ref.at[r], ab.at[x, z, 1 - r], sib_send, sib_recv, sib).wait_recv()
+    for n in range(2):
+        pl.when(r != n)(functools.partial(a_half_start, n))
     for d in (1, 3, 2):
         for n in range(2):
-            a_first(n, d, 0).start()
-    for n in range(2):
-        for d in (1, 3, 2):
             a_first(n, d, d).wait_recv()
-        for d in (1, 3):
-            a_second(n, d, 0).start()
+            a_second_start(n, d)
 
     def energies(h, c):
         for j in range(2 * RING):
@@ -247,14 +259,19 @@
         dtab[h] = pltpu.roll(dtab[h], phase, 1)
         return c
 
+    for h in range(IRREPS):
+        table_ref[h] = line_ref[h * VH : (h + 1) * VH].reshape(1, VH)
     lax.fori_loop(0, IRREPS, energies, 0)
-    for n in range(2):
-        for d in (1, 3):
-            a_second(n, d, d).wait_recv()
-            a_third(n, d, d).start()
-    for n in range(2):
-        for d in (1, 3):
-            a_third(n, d, 2).wait_recv()
+    for offset in (0, 1, 3, 2):
+        for n in range(2):
+            for d in (1, 3):
+                a_second(n, d, d, offset).wait_recv()
+                if offset in THIRD[d]:
+                    a_third(n, d, d, offset).start()
+    for d in (1, 3):
+        for offset in THIRD[d]:
+            for n in range(2):
+                a_third(n, d, 2, offset).wait_recv()
 
     lane_group = lax.div(lax.broadcasted_iota(jnp.int32, (BLOCK, LANES), 1), 16)
 
@@ -298,6 +315,13 @@
     def out_copy(p, t, peer):
         return snd.at[p, peer], o_ref.at[q * TILES + t]
 
+    def half_copy(p, t, peer):
+        return snd.at[p, peer, 0:HALVES], o_ref.at[q * TILES + t, 0:HALVES]
+
+    edge = (TILES - 1) * (1 - lax.rem(q, 2))
+    lane = lax.broadcasted_iota(jnp.int32, (8, LANES), 1)
+    kept = lax.div(lane, PAD) == lax.rem(q, 2)
+
     def step(p, carry):
         lo, hi = carry
         t = lax.rem(lo, 16)
@@ -335,12 +359,8 @@
         window = pl.ds(pl.multiple_of(t * LANES + PAD - phase, 16), LANES)
 
         def multiply(g, c):
-            total = lax.dot_general(
-                left[g, :, 0 : 2 * MAIN], wb[g, window, :], NT, preferred_element_type=F32
-            )
-            total = total + lax.dot_general(
-                left[g, :, 2 * MAIN :], wrb[window, :], NT, preferred_element_type=F32
-            )
+            right = jnp.concatenate([wb[g, window, :], wrb[window, :]], axis=1)
+            total = lax.dot_general(left[g], right, NT, preferred_element_type=F32)
             acc[g] = total.reshape(HALF, BLOCK, LANES)
             return c
 
@@ -366,12 +386,33 @@
             return c
 
         lax.fori_loop(0, IRREPS, finish, 0)
-        for ox, oz in SENDS:
-            peer = lax.rem(x + ox, 4) * 4 + lax.rem(z + oz, 4)
-            src, dst = out_copy(p, t, peer)
-            remote(src, dst, o_send.at[peer], o_recv.at[q], (r, peer * RING + y)).start()
-        src, dst = out_copy(p, t, q)
-        pltpu.make_async_copy(src, dst, o_send.at[q]).start()
+        @pl.when(t == edge)
+        def _():
+            def halve(peer, c):
+                for m in range(HALVES - 1):
+                    first = snd[p, peer, 2 * m].astype(F32)
+                    second = pltpu.roll(snd[p, peer, 2 * m + 1].astype(F32), PAD, 1)
+                    snd[p, peer, m] = jnp.where(kept, first, second).astype(BF16)
+                snd[p, peer, HALVES - 1] = snd[p, peer, ROWS - 1]
+                return c
+
+            lax.fori_loop(0, PLANE, halve, 0)
+            for ox, oz in SENDS:
+                peer = lax.rem(x + ox, 4) * 4 + lax.rem(z + oz, 4)
+                src, dst = half_copy(p, t, peer)
+                remote(src, dst, e_send.at[peer], e_recv.at[q], (r, peer * RING + y)).start()
+            src, dst = half_copy(p, t, q)
+            pltpu.make_async_copy(src, dst, e_send.at[q]).start()
+
+        @pl.when(t != edge)
+        def _():
+            for ox, oz in SENDS:
+                peer = lax.rem(x + ox, 4) * 4 + lax.rem(z + oz, 4)
+                src, dst = out_copy(p, t, peer)
+                remote(src, dst, o_send.at[peer], o_recv.at[q], (r, peer * RING + y)).start()
+            src, dst = out_copy(p, t, q)
+            pltpu.make_async_copy(src, dst, o_send.at[q]).start()
+
         return lax.div(lo, 16) + lax.rem(hi, 16) * 16**6, lax.div(hi, 16)
 
     lax.fori_loop(0, TILES, step, (lo, hi))
@@ -390,22 +431,33 @@
         for d in (1, 3, 2):
             a_first(n, d, 0).wait_send()
         for d in (1, 3):
-            a_second(n, d, 0).wait_send()
-            a_third(n, d, d).wait_send()
+            for offset in range(4):
+                a_second(n, d, 0, offset).wait_send()
+            for offset in THIRD[d]:
+                a_third(n, d, d, offset).wait_send()
 
     def all_tiles(peer):
-        return o_ref.at[pl.ds(peer * TILES, TILES)]
+        first = peer * TILES + lax.rem(peer, 2)
+        return o_ref.at[pl.ds(first, TILES - 1)]
+
+    def edge_tile(peer):
+        return o_ref.at[peer * TILES + (TILES - 1) * (1 - lax.rem(peer, 2)), 0:HALVES]
 
     def drain_out(o, c):
         peer = plane_peer(o)
-        whole = all_tiles(peer)
-        remote(whole, whole, o_send.at[peer], o_recv.at[peer], sib).wait_send()
-        remote(whole, whole, o_send.at[peer], o_recv.at[peer], sib).wait_recv()
+        whole, part = all_tiles(peer), edge_tile(peer)
+        for copy in (
+            remote(whole, whole, o_send.at[peer], o_recv.at[peer], sib),
+            remote(part, part, e_send.at[peer], e_recv.at[peer], sib),
+        ):
+            copy.wait_send()
+            copy.wait_recv()
         return c
 
     lax.fori_loop(1, PLANE, drain_out, 0)
-    own = all_tiles(q)
+    own, part = all_tiles(q), edge_tile(q)
     pltpu.make_async_copy(own, own, o_send.at[q]).wait()
+    pltpu.make_async_copy(part, part, e_send.at[q]).wait()
 
 
 def exchange(irrep, i, j, k, occ, virt, wm, wr, am):
@@ -426,19 +478,20 @@
             pltpu.VMEM((IRREPS, HALF, BLOCK, LANES), F32),
             pltpu.VMEM((TILES, PLANE, ROWS, 8, LANES), BF16),
             pltpu.VMEM((IRREPS, HALF, WIN), F32),
-            dma, dma, dma((3,)), dma((3, 2, 4)), dma((3, 2, 4)),
+            pltpu.VMEM((IRREPS, 1, VH), F32),
+            dma, dma, dma((3,)), dma((9, 2, 4)), dma((9, 2, 4)),
             dma((RING, 2, 2)), dma((RING, 2, 2)), dma((3,)), dma((3,)), dma((RING, 2, 2)), dma((RING, 2, 2)),
-            dma((PLANE,)), dma((PLANE,)),
+            dma((PLANE,)), dma((PLANE,)), dma((PLANE,)), dma((PLANE,)),
         ],
         compiler_params=pltpu.CompilerParams(
             collective_id=0, has_side_effects=True, vmem_limit_bytes=60 << 20
         ),
         name="exchange",
-    )(irrep, i, j, k, occ, virt, virt.reshape(IRREPS, 1, VH), wm, wr, am)
+    )(irrep, i, j, k, occ, virt, virt, wm, wr, am)
 
 
 def unpack_kernel(o_hbm, out_ref, o_ref, middle, sem, in_sem):
-    low = lax.broadcasted_iota(jnp.int32, (ROWS, 8, LANES), 2) < PAD
+    low = lax.broadcasted_iota(jnp.int32, (8, LANES), 1) < PAD
 
     def place(src, tile, n):
         lanes = pl.ds(pl.multiple_of(tile * LANES, LANES), LANES)
@@ -456,9 +509,12 @@
         for t in range(TILES - 1):
             place(o_ref.at[n * 2 * TILES + t], n * 25 + t, 0).start()
             place(o_ref.at[n * 2 * TILES + TILES + 1 + t], n * 25 + TILES + t, 0).start()
-        even = o_ref[n * 2 * TILES + TILES - 1].astype(F32)
-        odd = o_ref[n * 2 * TILES + TILES].astype(F32)
-        middle[n] = jnp.where(low, even, odd).astype(BF16)
+        for m in range(HALVES):
+            even = o_ref[n * 2 * TILES + TILES - 1, m].astype(F32)
+            odd = o_ref[n * 2 * TILES + TILES, m].astype(F32)
+            middle[n, 2 * m] = jnp.where(low, even, odd).astype(BF16)
+            if m < HALVES - 1:
+                middle[n, 2 * m + 1] = pltpu.roll(jnp.where(low, odd, even), PAD, 1).astype(BF16)
         place(middle.at[n], n * 25 + TILES - 1, 0).start()
         return c
 

time: 187 us -> 182 us (0.973)
  Pallas kernels: 181 us -> 179 us
    pallas_call x1, Pallas kernels: 168 us -> 166 us  [exchange(): pl.pallas_call(main_kernel, out_shape=jax.ShapeDtypeStruct((PLANE * TILES...]
where the time goes in v4:
time: 182 us; the launch traced here: 181 us
  Pallas kernels  179 us (98%)
    pallas_call x1, Pallas kernels, exchange(): pl.pallas_call(main_kernel, out_shape=jax.ShapeDtypeStruct((PLANE * TILES...  166 us
    pallas_call x1, Pallas kernels, unpack(): pl.pallas_call(unpack_kernel, out_shape=jax.ShapeDtypeStruct((ROWS, HALF,...  8.01 us
    pallas_call x1, Pallas kernels, pack(): pl.pallas_call(pack_kernel, out_shape=tuple((jax.ShapeDtypeStruct(shape,...  5.2 us

profile of v4, /device:TPU:1, one launch (start us, length us, event | category | flops | bytes accessed | tf_op | source)
XLA Modules:
  0.0 180.6 jit_solution(18349814815537555204)
XLA Ops:
  0.0 1.8 copy.9.a_ref
  1.8 5.2 %pack.1 = (bf16[8,400,384]{2,1,0:T(8,128)(2,1)}, bf16[400,128]{1,0:T(8,128)(2,1)}, bf16[2,79,8,128]{3,2,1,0:T(8,128)(2,1)}) custom-call(s32[200]{0:T(256)} %irrep_ref.3, s32[4]{0:T(128)} %k_ref.3, bf16[400,3200]{1,0:T(8,128)(2,1)} %bitcast.2, bf16[2,25,3200]{2,1,0:T(8,128)(2,1)} %copy.9.a_ref), custom_call_target="tpu_custom_call" | custom-call | tf_op jit(solution)/shard_map/pack/pallas_call | solution.py:88
  7.0 165.6 %exchange.1.o_hbm = bf16[208,25,8,128]{3,2,1,0:T(8,128)(2,1)} custom-call(s32[200]{0:T(256)} %irrep_ref.3, s32[16]{0:T(128)} %i_ref.1, s32[128]{0:T(128)} %j_ref.1, s32[4]{0:T(128)} %k_ref.3, f32[200]{0:T(256)} %occ_ref.1, f32[1600]{0:T(1024)} %line_ref.1, f32[1600]{0:T(1024)} %line_ref.1, bf16[8,400,384]{2,1,0:T(8,128)(2,1)} %get-tuple-element.8.wm_ref, ...), custom_call_target="tpu_custom_call" | custom-call | tf_op jit(solution)/shard_map/exchange/pallas_call | solution.py:468
  172.6 8.0 %unpack.1 = bf16[25,8,25600]{2,1,0:T(8,128)(2,1)} custom-call(bf16[208,25,8,128]{3,2,1,0:T(8,128)(2,1)} %exchange.1.o_hbm), custom_call_target="tpu_custom_call" | custom-call | tf_op jit(solution)/shard_map/unpack/pallas_call | solution.py:526

commit v5 on v4

--- a/solution.py
+++ b/solution.py
@@ -39,7 +39,7 @@
 
 
 def pack_kernel(
-    irrep_ref, k_ref, w_ref, a_ref, wm_ref, wr_ref, am_ref, wm, wr, am, rows, last, rest, sem
+    irrep_ref, k_ref, w_ref, a_ref, wm_ref, wr_ref, am_ref, wm, wr, am, wide, rows, last, rest, sem
 ):
     r = lax.axis_index("rep")
     for k in range(2):
@@ -59,12 +59,14 @@
     ]
     copies[0].start()
     copies[1].start()
+    for k in range(2):
+        wide[k, 0:ROWS, :] = a_ref[:, k, :].astype(F32)
     for half in range(2):
         rest[...] = jnp.zeros_like(rest)
         for i in range(HALF):
             first = (half * HALF + i) * VH
-            rows[0:ROWS, 0:VH] = a_ref[0, :, first : first + VH].astype(F32)
-            rows[0:ROWS, VH:COLS] = a_ref[1, :, first : first + VH].astype(F32)
+            rows[0:ROWS, 0:VH] = wide[0, 0:ROWS, first : first + VH]
+            rows[0:ROWS, VH:COLS] = wide[1, 0:ROWS, first : first + VH]
             for lt in range(3):
                 lanes = slice(lt * LANES, (lt + 1) * LANES)
                 am[half, lt * 25 + 3 * i : lt * 25 + 3 * i + 3] = (
@@ -92,6 +94,7 @@
         out_specs=(hbm, hbm, hbm),
         scratch_shapes=[
             *(pltpu.VMEM(shape, BF16) for shape in shapes),
+            pltpu.VMEM((2, 32, a.shape[2]), F32),
             pltpu.VMEM((32, 512), F32),
             pltpu.VMEM((3, 8, LANES), F32),
             pltpu.VMEM((32, LANES), F32),
@@ -542,7 +545,7 @@
 def per_device(
     amplitudes, intermediate, occ_irrep, i_window, j_window, k_window, occ_energy, virt_energy
 ):
-    wm, wr, am = pack(occ_irrep, k_window, intermediate.reshape(COLS, -1), amplitudes)
+    wm, wr, am = pack(occ_irrep, k_window, intermediate.reshape(COLS, -1), amplitudes.transpose(1, 0, 2))
     o = exchange(
         occ_irrep, i_window, j_window, k_window, occ_energy, virt_energy, wm, wr, am
     )

time: 182 us -> 179 us (0.984)
  no operation moved by 1% of the time
where the time goes in v5:
time: 179 us
  Pallas kernels  179 us (100%)
    pallas_call x1, Pallas kernels, exchange(): pl.pallas_call(main_kernel, out_shape=jax.ShapeDtypeStruct((PLANE * TILES...  165 us
    pallas_call x1, Pallas kernels, unpack(): pl.pallas_call(unpack_kernel, out_shape=jax.ShapeDtypeStruct((ROWS, HALF,...  8.01 us
    pallas_call x1, Pallas kernels, pack(): pl.pallas_call(pack_kernel, out_shape=tuple((jax.ShapeDtypeStruct(shape,...  5.31 us

profile of v5, /device:TPU:1, one launch (start us, length us, event | category | flops | bytes accessed | tf_op | source)
XLA Modules:
  0.0 178.8 jit_solution(8646295803154959953)
XLA Ops:
  0.0 5.3 %pack.1 = (bf16[8,400,384]{2,1,0:T(8,128)(2,1)}, bf16[400,128]{1,0:T(8,128)(2,1)}, bf16[2,79,8,128]{3,2,1,0:T(8,128)(2,1)}) custom-call(s32[200]{0:T(256)} %irrep_ref.3, s32[4]{0:T(128)} %k_ref.3, bf16[400,3200]{1,0:T(8,128)(2,1)} %bitcast.3, bf16[25,2,3200]{2,1,0:T(2,128)(2,1)} %bitcast.4), custom_call_target="tpu_custom_call" | custom-call | tf_op jit(solution)/shard_map/pack/pallas_call | solution.py:90
  5.3 165.5 %exchange.1.o_hbm = bf16[208,25,8,128]{3,2,1,0:T(8,128)(2,1)} custom-call(s32[200]{0:T(256)} %irrep_ref.3, s32[16]{0:T(128)} %i_ref.1, s32[128]{0:T(128)} %j_ref.1, s32[4]{0:T(128)} %k_ref.3, f32[200]{0:T(256)} %occ_ref.1, f32[1600]{0:T(1024)} %line_ref.1, f32[1600]{0:T(1024)} %line_ref.1, bf16[8,400,384]{2,1,0:T(8,128)(2,1)} %get-tuple-element.8.wm_ref, ...), custom_call_target="tpu_custom_call" | custom-call | tf_op jit(solution)/shard_map/exchange/pallas_call | solution.py:471
  170.8 8.0 %unpack.1 = bf16[25,8,25600]{2,1,0:T(8,128)(2,1)} custom-call(bf16[208,25,8,128]{3,2,1,0:T(8,128)(2,1)} %exchange.1.o_hbm), custom_call_target="tpu_custom_call" | custom-call | tf_op jit(solution)/shard_map/unpack/pallas_call | solution.py:529

commit v6 on v5

--- a/solution.py
+++ b/solution.py
@@ -25,10 +25,10 @@
 F32 = jnp.float32
 BF16 = jnp.bfloat16
 ORDER = (
-    (1, 2, 3, 4, 11, 0, 5, 10, 12, 6, 7, 8, 9),
-    (4, 5, 3, 2, 6, 7, 0, 1, 8, 9, 10, 11, 12),
+    (1, 2, 3, 4, 11, 0, 12, 5, 10, 6, 7, 8, 9),
+    (4, 5, 3, 2, 6, 7, 1, 8, 0, 12, 9, 10, 11),
     (7, 8, 6, 5, 9, 10, 4, 11, 12, 0, 1, 2, 3),
-    (10, 11, 12, 9, 8, 0, 1, 7, 2, 3, 4, 5, 6),
+    (10, 11, 9, 8, 1, 0, 12, 7, 2, 3, 4, 5, 6),
 )
 PARTS = {1: ((144, 256), (0, 144)), 3: ((0, 256), (256, 144))}
 THIRD = {1: (0, 3), 3: (1, 2)}

time: 179 us -> 179 us (level)
  no operation moved by 1% of the time
where the time goes in v6:
time: 179 us
  Pallas kernels  179 us (100%)
    pallas_call x1, Pallas kernels, exchange(): pl.pallas_call(main_kernel, out_shape=jax.ShapeDtypeStruct((PLANE * TILES...  166 us
    pallas_call x1, Pallas kernels, unpack(): pl.pallas_call(unpack_kernel, out_shape=jax.ShapeDtypeStruct((ROWS, HALF,...  8.01 us
    pallas_call x1, Pallas kernels, pack(): pl.pallas_call(pack_kernel, out_shape=tuple((jax.ShapeDtypeStruct(shape,...  5.31 us

profile of v6, /device:TPU:1, one launch (start us, length us, event | category | flops | bytes accessed | tf_op | source)
XLA Modules:
  0.0 179.2 jit_solution(2127308097373393858)
XLA Ops:
  0.0 5.3 %pack.1 = (bf16[8,400,384]{2,1,0:T(8,128)(2,1)}, bf16[400,128]{1,0:T(8,128)(2,1)}, bf16[2,79,8,128]{3,2,1,0:T(8,128)(2,1)}) custom-call(s32[200]{0:T(256)} %irrep_ref.3, s32[4]{0:T(128)} %k_ref.3, bf16[400,3200]{1,0:T(8,128)(2,1)} %bitcast.3, bf16[25,2,3200]{2,1,0:T(2,128)(2,1)} %bitcast.4), custom_call_target="tpu_custom_call" | custom-call | tf_op jit(solution)/shard_map/pack/pallas_call | solution.py:90
  5.3 165.8 %exchange.1.o_hbm = bf16[208,25,8,128]{3,2,1,0:T(8,128)(2,1)} custom-call(s32[200]{0:T(256)} %irrep_ref.3, s32[16]{0:T(128)} %i_ref.1, s32[128]{0:T(128)} %j_ref.1, s32[4]{0:T(128)} %k_ref.3, f32[200]{0:T(256)} %occ_ref.1, f32[1600]{0:T(1024)} %line_ref.1, f32[1600]{0:T(1024)} %line_ref.1, bf16[8,400,384]{2,1,0:T(8,128)(2,1)} %get-tuple-element.8.wm_ref, ...), custom_call_target="tpu_custom_call" | custom-call | tf_op jit(solution)/shard_map/exchange/pallas_call | solution.py:471
  171.2 8.0 %unpack.1 = bf16[25,8,25600]{2,1,0:T(8,128)(2,1)} custom-call(bf16[208,25,8,128]{3,2,1,0:T(8,128)(2,1)} %exchange.1.o_hbm), custom_call_target="tpu_custom_call" | custom-call | tf_op jit(solution)/shard_map/unpack/pallas_call | solution.py:529

commit v7 on v6

--- a/solution.py
+++ b/solution.py
@@ -504,11 +504,12 @@
         part = pl.ds(n * 2 * TILES, 2 * TILES)
         return pltpu.make_async_copy(o_hbm.at[part], o_ref.at[part], in_sem.at[n])
 
-    for n in range(PLANE // 2):
+    for n in range(2):
         load(n).start()
 
     def pair(n, c):
         load(n).wait()
+        pl.when(n + 2 < PLANE // 2)(lambda: load(n + 2).start())
         for t in range(TILES - 1):
             place(o_ref.at[n * 2 * TILES + t], n * 25 + t, 0).start()
             place(o_ref.at[n * 2 * TILES + TILES + 1 + t], n * 25 + TILES + t, 0).start()

time: 179 us -> 181 us (1.011)
  Pallas kernels: 179 us -> 181 us
    pallas_call x1, Pallas kernels: 8.01 us -> 9.85 us  [unpack(): pl.pallas_call(unpack_kernel, out_shape=jax.ShapeDtypeStruct((ROWS, HALF,...]
where the time goes in v7:
time: 181 us
  Pallas kernels  181 us (100%)
    pallas_call x1, Pallas kernels, exchange(): pl.pallas_call(main_kernel, out_shape=jax.ShapeDtypeStruct((PLANE * TILES...  166 us
    pallas_call x1, Pallas kernels, unpack(): pl.pallas_call(unpack_kernel, out_shape=jax.ShapeDtypeStruct((ROWS, HALF,...  9.85 us
    pallas_call x1, Pallas kernels, pack(): pl.pallas_call(pack_kernel, out_shape=tuple((jax.ShapeDtypeStruct(shape,...  5.31 us

profile of v7, /device:TPU:1, one launch (start us, length us, event | category | flops | bytes accessed | tf_op | source)
XLA Modules:
  0.0 181.0 jit_solution(1308447707190602512)
XLA Ops:
  0.0 5.3 %pack.1 = (bf16[8,400,384]{2,1,0:T(8,128)(2,1)}, bf16[400,128]{1,0:T(8,128)(2,1)}, bf16[2,79,8,128]{3,2,1,0:T(8,128)(2,1)}) custom-call(s32[200]{0:T(256)} %irrep_ref.3, s32[4]{0:T(128)} %k_ref.3, bf16[400,3200]{1,0:T(8,128)(2,1)} %bitcast.3, bf16[25,2,3200]{2,1,0:T(2,128)(2,1)} %bitcast.4), custom_call_target="tpu_custom_call" | custom-call | tf_op jit(solution)/shard_map/pack/pallas_call | solution.py:90
  5.3 165.8 %exchange.1.o_hbm = bf16[208,25,8,128]{3,2,1,0:T(8,128)(2,1)} custom-call(s32[200]{0:T(256)} %irrep_ref.3, s32[16]{0:T(128)} %i_ref.1, s32[128]{0:T(128)} %j_ref.1, s32[4]{0:T(128)} %k_ref.3, f32[200]{0:T(256)} %occ_ref.1, f32[1600]{0:T(1024)} %line_ref.1, f32[1600]{0:T(1024)} %line_ref.1, bf16[8,400,384]{2,1,0:T(8,128)(2,1)} %get-tuple-element.8.wm_ref, ...), custom_call_target="tpu_custom_call" | custom-call | tf_op jit(solution)/shard_map/exchange/pallas_call | solution.py:471
  171.2 9.9 %unpack.1 = bf16[25,8,25600]{2,1,0:T(8,128)(2,1)} custom-call(bf16[208,25,8,128]{3,2,1,0:T(8,128)(2,1)} %exchange.1.o_hbm), custom_call_target="tpu_custom_call" | custom-call | tf_op jit(solution)/shard_map/unpack/pallas_call | solution.py:530
